TPU v7x, 256 devices: a whole 4x4x8 slice. The times are simulated.
256 devices in a mesh: expert: 64 (over z, x, core), mp: 4 (over y).
Axes of the slice: x: 4, y: 4, z: 8, core: 2. Of those that a mesh axis runs over, the one named last changes fastest.
Arguments:
- hidden_state: bfloat16 [8192, 2048], P('expert', 'mp'), as said below
- context: bfloat16 [8192, 2048], P('expert', 'mp'), may hold values from -6 to 6
- out_proj: bfloat16 [2048, 2048], P('mp', 'expert'), may hold values from -0.125 to 0.125
- norm_gain: bfloat16 [2048], P('mp'), may hold values from 0.25 to 1.75
- router_weight: float32 [2048, 64], P('mp'), as said below
- expert_in: bfloat16 [64, 2048, 2, 1408], P('expert', None, None, 'mp'), may hold values from -0.125 to 0.125
- expert_out: bfloat16 [64, 1408, 2048], P('expert', 'mp'), may hold values from -0.15625 to 0.15625
- shared_in: bfloat16 [2048, 2, 2816], P('expert', None, 'mp'), may hold values from -0.125 to 0.125
- shared_out: bfloat16 [2816, 2048], P('mp', 'expert'), may hold values from -0.109375 to 0.109375
- route_ids: int32 [8192, 6], P('expert'), may hold values from 0 to 63, all different within a row; in each aligned block of 128 rows (0 to 127, 128 to 255, ...) at most 20 rows name the same one
Outputs:
- output: float32 [8192, 2048], P('expert', 'mp')
Inputs may be any that keep to these rules, and one draw needn't show every extreme that they name: `route_ids`: each row names 6 different experts; among the rows of one index of the expert axis no expert is named by more than 20 rows. `router_weight`: finite float32 router columns; no range is promised. `hidden_state`: finite values; no range is promised.
All inputs are finite; a program needn't handle non-finite values.
Results may differ from a plain program's by a relative error of at most 0.0025.
Values may be sent and summed in bfloat16 or wider, within the bound.
A program may use at most 128 MiB of HBM per device.

v0:
```python
import jax
import jax.numpy as jnp
from jax import lax
from jax.sharding import PartitionSpec as P


def per_device(
    hidden_state,
    context,
    out_proj,
    norm_gain,
    router_weight,
    expert_in,
    expert_out,
    shared_in,
    shared_out,
    route_ids,
):
    rows_here, top = route_ids.shape
    experts = router_weight.shape[1]
    width = out_proj.shape[0] * lax.axis_size("mp")
    capacity = max(2, min(rows_here, rows_here * top // experts * 5 // 3))
    partial_attn = jnp.dot(
        context,
        lax.all_gather(out_proj, "expert", axis=1, tiled=True),
        preferred_element_type=jnp.float32,
    )
    attn = lax.psum_scatter(partial_attn, "mp", scatter_dimension=1, tiled=True)
    mixed = hidden_state.astype(jnp.float32) + attn
    gain = norm_gain.astype(jnp.float32)
    squares = lax.psum(jnp.sum(mixed * mixed, axis=1), "mp")
    inverse = lax.rsqrt(squares / width + 1e-06)[:, None]
    normed32 = mixed * inverse * gain
    logits = lax.psum(jnp.dot(normed32, router_weight, precision=lax.Precision.HIGHEST), "mp")
    normed = normed32.astype(jnp.bfloat16)
    gates = jax.nn.softmax(jnp.take_along_axis(logits, route_ids, axis=1), axis=1)
    full_rows = lax.all_gather(normed, "mp", axis=1, tiled=True)
    shared_width = shared_in.shape[2]
    piece = lax.all_gather(shared_in, "expert", axis=0, tiled=True)
    shared_both = jnp.dot(
        full_rows,
        piece.reshape(piece.shape[0], 2 * shared_width),
        preferred_element_type=jnp.float32,
    )
    shared_both = shared_both.reshape(rows_here, 2, shared_width)
    shared_hidden = (jax.nn.silu(shared_both[:, 0]) * shared_both[:, 1]).astype(jnp.bfloat16)
    shared_part = jnp.dot(
        shared_hidden,
        lax.all_gather(shared_out, "expert", axis=1, tiled=True),
        preferred_element_type=jnp.float32,
    )
    flat = route_ids.reshape(-1)
    onehot = (flat[:, None] == jnp.arange(experts, dtype=jnp.int32)[None, :]).astype(jnp.int32)
    position = jnp.sum(onehot * jnp.cumsum(onehot, axis=0), axis=1) - 1
    slot_of = flat * capacity + position
    source = (
        jnp.zeros((experts * capacity,), jnp.int32)
        .at[slot_of]
        .set(jnp.arange(flat.shape[0], dtype=jnp.int32) // top)
    )
    filled = jnp.zeros((experts * capacity,), jnp.bool_).at[slot_of].set(True)
    outgoing = jnp.where(filled[:, None], normed[source], jnp.zeros((), jnp.bfloat16)).reshape(
        experts, capacity, normed.shape[1]
    )
    quarter = expert_in.shape[3]
    weights_in = expert_in[0].reshape(width, 2 * quarter)
    incoming = lax.all_to_all(outgoing, "expert", split_axis=0, concat_axis=0, tiled=True)
    sources = incoming.shape[0]
    items = incoming.shape[1]
    gathered = lax.all_gather(incoming, "mp", axis=2, tiled=True).reshape(sources * items, width)
    inner = jnp.dot(gathered, weights_in, preferred_element_type=jnp.float32).reshape(
        -1, 2, quarter
    )
    hidden = (jax.nn.silu(inner[:, 0]) * inner[:, 1]).astype(jnp.bfloat16)
    partial_out = jnp.dot(hidden, expert_out[0], preferred_element_type=jnp.float32).astype(
        jnp.bfloat16
    )
    partial_out = partial_out.reshape(sources, items, width)
    result = lax.all_to_all(partial_out, "expert", split_axis=0, concat_axis=0, tiled=True)
    picked = result.reshape(experts * capacity, result.shape[2])[slot_of]
    slot_total = lax.psum_scatter(
        lax.optimization_barrier(picked).astype(jnp.float32).astype(jnp.bfloat16),
        "mp",
        scatter_dimension=1,
        tiled=True,
    )
    expert_sum = lax.optimization_barrier(slot_total).astype(jnp.float32)
    expert_sum = expert_sum.reshape(rows_here, top, expert_sum.shape[1])
    routed = jnp.sum(gates[:, :, None] * expert_sum, axis=1)
    shared = lax.psum_scatter(shared_part, "mp", scatter_dimension=1, tiled=True)
    return mixed + routed + shared


def solution(mesh):
    return jax.shard_map(
        per_device,
        mesh=mesh,
        in_specs=(
            P("expert", "mp"),
            P("expert", "mp"),
            P("mp", "expert"),
            P("mp"),
            P("mp", None),
            P("expert", None, None, "mp"),
            P("expert", "mp", None),
            P("expert", None, "mp"),
            P("mp", "expert"),
            P("expert", None),
        ),
        out_specs=P("expert", "mp"),
        check_vma=False,
    )
```

profile of v0, /device:TPU:1, one launch (start us, length us, event | category | flops | bytes accessed | tf_op | source)
XLA Modules:
  0.0 545.3 jit_solution(8072217353120096807)
XLA Ops:
  7.3 84.3 %all-gather.5.cloned.1.call-done = bf16[512,2048]{0,1:T(8,128)(2,1)} async-done(((bf16[512,32]{0,1:T(8,128)(2,1)}), bf16[512,2048]{0,1:T(8,128)(2,1)}) %all-gather.5.cloned.1.call-update) | async-done | bytes 2097168 | tf_op jit(solution)/shard_map/all_gather | solution.py:25
  91.6 3.5 fusion.34
  98.1 3.4 scatter_custom_fusion.1
  101.5 3.4 scatter_custom_fusion
  105.1 12.2 %reduce-scatter.4.cloned.1.call-done = f32[128,512]{1,0:T(8,128)} async-done(((f32[128,2048]{1,0:T(8,128)}), f32[128,512]{1,0:T(8,128)}) %reduce-scatter.4.cloned.1.call-update) | async-done | bytes 262160 | tf_op jit(solution)/shard_map/reduce_scatter | solution.py:28
  118.3 6.6 %psum.14 = f32[128]{0:T(128)S(1)} all-reduce(f32[128]{0:T(128)S(1)} %multiply_reduce_fusion.1), channel_id=1, replica_groups=mesh['expert'=64,'mp'=4] {'mp'}, use_global_device_ids=true, to_apply=%region_2.0 | all-reduce | flops 128 | bytes 1024 | tf_op jit(solution)/shard_map/psum | solution.py:31
  126.0 4.7 gather_fusion
  135.6 52.8 %all_to_all.10 = bf16[64,20,512]{2,1,0:T(8,128)(2,1)} all-to-all(bf16[64,20,512]{2,1,0:T(8,128)(2,1)S(1)} %broadcast_select_fusion), channel_id=1, replica_groups=mesh['expert'=64,'mp'=4] {'expert'}, dimensions={0} | all-to-all | bytes 2621440 | tf_op jit(solution)/shard_map/all_to_all | solution.py:67
  189.0 63.2 %all-gather.7.cloned.1.call-done = bf16[64,20,2048]{2,1,0:T(8,128)(2,1)} async-done(((bf16[64,20,512]{2,1,0:T(8,128)(2,1)}), bf16[64,20,2048]{2,1,0:T(8,128)(2,1)}) %all-gather.7.cloned.1.call-update) | async-done | bytes 5242896 | tf_op jit(solution)/shard_map/all_gather | solution.py:70
  252.3 9.0 %reshape.167 = bf16[1280,2048,1]{1,0,2:T(8,128)(2,1)} reshape(bf16[64,20,2048]{2,1,0:T(8,128)(2,1)} %all-gather.7.cloned.1.call-done) | data formatting | bytes 10485760 | tf_op jit(solution)/shard_map/reshape | solution.py:70
  261.2 6.5 %fusion.2 = f32[1280,2,352]{0,2,1:T(8,128)S(1)} fusion(bf16[1280,2048,1]{1,0,2:T(8,128)(2,1)} %reshape.167, bf16[1,2048,2,352]{1,3,2,0:T(8,128)(2,1)S(1)} %copy-done), kind=kOutput, calls=%fused_computation.8 | convolution fusion | flops 3690987520 | bytes 11730944 | tf_op jit(solution)/shard_map/dot_general | solution.py:71
  267.8 4.7 convolution_convert_fusion
  272.5 8.9 %reshape.116 = bf16[64,20,2048]{2,1,0:T(8,128)(2,1)} reshape(bf16[1280,2048]{1,0:T(8,128)(2,1)} %convolution_convert_fusion) | data formatting | bytes 10485760 | tf_op jit(solution)/shard_map/reshape | solution.py:78
  281.4 10.8 %all-to-all-start.1 = ((bf16[64,20,2048]{2,1,0:T(8,128)(2,1)}), bf16[64,20,2048]{2,1,0:T(8,128)(2,1)}, u32[]{:S(2)}, u32[]{:S(2)}) async-start(bf16[64,20,2048]{2,1,0:T(8,128)(2,1)} %reshape.116), calls=%async_computation.2 | async-start | bytes 12582912 | tf_op jit(solution)/shard_map/all_to_all | solution.py:79
  292.9 157.8 %all-to-all-done.1 = bf16[64,20,2048]{2,1,0:T(8,128)(2,1)} async-done(((bf16[64,20,2048]{2,1,0:T(8,128)(2,1)}), bf16[64,20,2048]{2,1,0:T(8,128)(2,1)}, u32[]{:S(2)}, u32[]{:S(2)}) %all-to-all-start.1) | async-done | bytes 5242912 | tf_op jit(solution)/shard_map/all_to_all | solution.py:79
  450.7 9.0 %reshape.117 = bf16[1280,2048]{1,0:T(8,128)(2,1)} reshape(bf16[64,20,2048]{2,1,0:T(8,128)(2,1)} %all-to-all-done.1) | data formatting | bytes 10485760 | tf_op jit(solution)/shard_map/reshape | solution.py:80
  459.7 10.3 %gather_fusion.1 = bf16[768,2048]{1,0:T(8,128)(2,1)} fusion(bf16[1280,2048]{1,0:T(8,128)(2,1)} %reshape.117, s32[1024]{0:T(1024)S(1)} %pad_clamp_fusion.1), kind=kCustom, calls=%fused_computation.1 | custom fusion | bytes 6294528 | tf_op jit(solution)/shard_map/gather | solution.py:80
  470.1 10.6 %all_gather.17 = bf16[128,2048]{1,0:T(8,128)(2,1)S(1)} all-gather(bf16[128,512]{1,0:T(8,128)(2,1)S(1)} %fusion.11), channel_id=1, replica_groups=mesh['expert'=64,'mp'=4] {'mp'}, dimensions={1}, use_global_device_ids=true | all-gather | bytes 655360 | tf_op jit(solution)/shard_map/all_gather | solution.py:37
  480.7 16.2 %copy.40 = bf16[2048,2,704]{0,2,1:T(8,128)(2,1)} copy(bf16[2048,2,704]{2,1,0:T(2,128)(2,1)} %all-gather.9.cloned.1.call-done) | data formatting | bytes 11534336 | tf_op jit(solution)/shard_map/all_gather | solution.py:39
  496.8 4.4 fusion
  501.3 4.1 fusion.16
  506.2 12.5 %psum.15 = f32[128,64]{0,1:T(8,128)S(1)} all-reduce(f32[128,64]{0,1:T(8,128)S(1)} %fusion.12), channel_id=1, replica_groups=mesh['expert'=64,'mp'=4] {'mp'}, use_global_device_ids=true, to_apply=%region_3.0 | all-reduce | flops 8192 | bytes 65536 | tf_op jit(solution)/shard_map/psum | solution.py:34
  518.7 5.1 gather_fusion.2
  529.8 6.9 %reduce-scatter.8.cloned.1.call-done = f32[128,512]{1,0:T(8,128)} async-done(((f32[128,2048]{1,0:T(8,128)}), f32[128,512]{1,0:T(8,128)}) %reduce-scatter.8.cloned.1.call-update) | async-done | bytes 262160 | tf_op jit(solution)/shard_map/reduce_scatter | solution.py:90
  (71 shorter events, 20.6 us)
Async XLA Ops:
  6.5 254.7 %copy-start = (bf16[1,2048,2,352]{1,3,2,0:T(8,128)(2,1)S(1)}, bf16[1,2048,2,352]{1,3,2,0:T(8,128)(2,1)}, u32[]{:S(2)}) copy-start(bf16[1,2048,2,352]{1,3,2,0:T(8,128)(2,1)} %param.15) | copy-start | bytes 8650756
  6.5 88.6 %copy-start.4 = (s32[128,6]{0,1:T(8,128)S(1)}, s32[128,6]{0,1:T(8,128)}, u32[]{:S(2)}) copy-start(s32[128,6]{0,1:T(8,128)} %param.19) | copy-start | bytes 9220
  6.5 89.0 %copy-start.6 = (bf16[512]{0:T(512)(128)(2,1)S(1)}, bf16[512]{0:T(512)(128)(2,1)}, u32[]{:S(2)}) copy-start(bf16[512]{0:T(512)(128)(2,1)} %param.13) | copy-start | bytes 3076
  6.5 85.0 %all-gather.5.cloned.1.call-start = ((), (), s32[]{:S(2)}) async-start(), calls=%async_computation.5 | async-start | bytes 2129920 | tf_op jit(solution)/shard_map/all_gather | solution.py:25
  7.3 109.9 %copy-start.3 = (bf16[128,512]{1,0:T(8,128)(2,1)S(1)}, bf16[128,512]{1,0:T(8,128)(2,1)}, u32[]{:S(2)}) copy-start(bf16[128,512]{1,0:T(8,128)(2,1)} %param.10) | copy-start | bytes 393220
  7.3 109.9 %reduce-scatter.4.cloned.1.call-start = ((), (), s32[]{:S(2)}) async-start(), calls=%async_computation.6 | async-start | bytes 1310720 | tf_op jit(solution)/shard_map/reduce_scatter | solution.py:28
  95.1 157.2 %all-gather.7.cloned.1.call-start = ((), (), s32[]{:S(2)}) async-start(), calls=%async_computation.7 | async-start | bytes 7864320 | tf_op jit(solution)/shard_map/all_gather | solution.py:70
  188.5 292.2 %all-gather.9.cloned.1.call-start = ((), (), s32[]{:S(2)}) async-start(), calls=%async_computation.9 | async-start | bytes 6389760 | tf_op jit(solution)/shard_map/all_gather | solution.py:39
  261.2 6.5 %copy-start.7 = (bf16[1,352,2048]{2,1,0:T(8,128)(2,1)S(1)}, bf16[1,352,2048]{2,1,0:T(8,128)(2,1)}, u32[]{:S(2)}) copy-start(bf16[1,352,2048]{2,1,0:T(8,128)(2,1)} %param.16) | copy-start | bytes 4325380
  281.4 169.3 %all-to-all-start.1 = ((bf16[64,20,2048]{2,1,0:T(8,128)(2,1)}), bf16[64,20,2048]{2,1,0:T(8,128)(2,1)}, u32[]{:S(2)}, u32[]{:S(2)}) async-start(bf16[64,20,2048]{2,1,0:T(8,128)(2,1)} %reshape.116), calls=%async_computation.2 | async-start | bytes 12582912 | tf_op jit(solution)/shard_map/all_to_all | solution.py:79
  292.3 209.0 %all-gather.11.cloned.1.call-start = ((), (), s32[]{:S(2)}) async-start(), calls=%async_computation.10 | async-start | bytes 3194880 | tf_op jit(solution)/shard_map/all_gather | solution.py:49
  292.9 232.0 %reduce-scatter.6.cloned.1.call-start = ((), (), s32[]{:S(2)}) async-start(), calls=%async_computation.8 | async-start | bytes 3932160 | tf_op jit(solution)/shard_map/reduce_scatter | solution.py:81
  470.0 66.7 %reduce-scatter.8.cloned.1.call-start = ((), (), s32[]{:S(2)}) async-start(), calls=%async_computation.11 | async-start | bytes 1310720 | tf_op jit(solution)/shard_map/reduce_scatter | solution.py:90
  501.2 4.4 copy-start.2
  501.2 4.4 copy-start.5
  524.1 14.4 %copy-start.1 = (bf16[1,2048,2,352]{1,3,2,0:T(8,128)(2,1)S(1)}, bf16[1,2048,2,352]{1,3,2,0:T(8,128)(2,1)}, u32[]{:S(2)}) copy-start(bf16[1,2048,2,352]{1,3,2,0:T(8,128)(2,1)} %param.15) | copy-start | bytes 8650756
Sparse Core Ops, SparseCore 0:
  10.1 81.3 all-gather.4
  95.2 21.9 reduce-scatter.3
  188.6 63.6 all-gather.6
  255.2 113.6 all-gather.8
  371.9 92.5 all-gather.10
  470.1 40.6 reduce-scatter.5
  513.5 23.1 reduce-scatter.7
where the time goes:
time: 549 us; the launch traced here: 545 us
  waiting for transfers between devices  326 us (59%)
  blocking collectives  82.6 us (15%)
  local copies, waits for them, and re-layouts  78.1 us (14%)
  matrix products  23.6 us (4%)
  between operations  13.8 us (3%)
  starting transfers between devices  11.2 us (2%)
  other arithmetic  9.94 us (2%)
    all_to_all x1, waiting for transfers between devices, per_device(): lax.all_to_all(partial_out, 'expert', split_axis=0, concat_axis=0, tiled=...  158 us
    all_gather x1, waiting for transfers between devices, per_device(): lax.all_gather(out_proj, 'expert', axis=1, tiled=True)  84.3 us
    all_gather x1, waiting for transfers between devices, per_device(): lax.all_gather(incoming, 'mp', axis=2, tiled=True)  63.2 us
    all_to_all x1, blocking collectives, per_device(): lax.all_to_all(outgoing, 'expert', split_axis=0, concat_axis=0, tiled=True)  52.8 us
    all_gather x1, local copies, waits for them, and re-layouts, per_device(): piece = lax.all_gather(shared_in, 'expert', axis=0, tiled=True)  16.2 us
    psum x1, blocking collectives, per_device(): lax.psum(jnp.dot(normed32, router_weight, precision=lax.Precision.HIGHEST...  12.5 us
    reduce_scatter x1, waiting for transfers between devices, per_device(): attn = lax.psum_scatter(partial_attn, 'mp', scatter_dimension=1, tiled=True)  12.2 us
  transfers between devices with their start and end apart: 8, of which 5 were waited for; matrix products, arithmetic and copies ran while one was open for 17% of the time, Pallas kernels for 0%

commit v1 on v0

v1 whole, which is shorter than its diff:
```python
import jax
import jax.numpy as jnp
from jax import lax
from jax.experimental import pallas as pl
from jax.experimental.pallas import tpu as pltpu
from jax.sharding import PartitionSpec as P

NZ, NX, NC, NY = 8, 4, 2, 4
NE = NZ * NX * NC
ROWS, FEAT, WIDTH = 128, 512, 2048
TOP, CAP, SLOT = 6, 20, 32
QUARTER, QPAD = 352, 384
SWIDTH, SPAD = 704, 768
CHUNK = NX * NC * CAP
HALF = CHUNK // 2
NCH = NZ + 1
F32, BF16 = jnp.float32, jnp.bfloat16
VMEM_LIMIT = 64 * 1024 * 1024 - 65536


def coords():
    e = lax.axis_index("expert")
    y = lax.axis_index("mp")
    z = lax.div(e, NX * NC)
    x = lax.rem(lax.div(e, NC), NX)
    c = lax.rem(e, NC)
    return e, z, x, c, y


def eid(z, x, c):
    return z * (NX * NC) + x * NC + c


def blk(z, c, x):
    return z * (NX * NC) + c * NX + x


def send(src, dst, ssem, rsem, e, y):
    return pltpu.make_async_remote_copy(
        src_ref=src,
        dst_ref=dst,
        send_sem=ssem,
        recv_sem=rsem,
        device_id={"expert": e, "mp": y},
        device_id_type=pl.DeviceIdType.MESH,
    )


def greet(e, y):
    pl.semaphore_signal(
        pltpu.get_barrier_semaphore(),
        inc=1,
        device_id={"expert": e, "mp": y},
        device_id_type=pl.DeviceIdType.MESH,
    )


def nt(a, b):
    return lax.dot_general(a, b, (((1,), (1,)), ((), ())), preferred_element_type=F32)


class XGather:
    def __init__(self, src, buf, own, lft, rgt, opp, half, ssem, rsem, to_r, to_l, y):
        self.own_r = send(src, buf.at[own], ssem.at[0], rsem.at[0], to_r, y)
        self.own_l = send(src, buf.at[own], ssem.at[1], rsem.at[1], to_l, y)
        lo, hi = pl.ds(0, half), pl.ds(half, half)
        self.got_l = send(src, buf.at[lft], ssem.at[0], rsem.at[0], to_r, y)
        self.got_r = send(src, buf.at[rgt], ssem.at[1], rsem.at[1], to_l, y)
        self.fwd_r = send(buf.at[lft, lo], buf.at[lft, lo], ssem.at[2], rsem.at[2], to_r, y)
        self.fwd_l = send(buf.at[rgt, hi], buf.at[rgt, hi], ssem.at[3], rsem.at[3], to_l, y)
        self.end_r = send(buf.at[opp, lo], buf.at[opp, lo], ssem.at[2], rsem.at[2], to_r, y)
        self.end_l = send(buf.at[opp, hi], buf.at[opp, hi], ssem.at[3], rsem.at[3], to_l, y)

    def start(self):
        self.own_r.start()
        self.own_l.start()

    def forward(self):
        self.got_l.wait_recv()
        self.fwd_r.start()
        self.got_r.wait_recv()
        self.fwd_l.start()

    def finish(self):
        self.end_r.wait_recv()
        self.end_l.wait_recv()

    def drain(self):
        for copy in (self.own_r, self.own_l, self.fwd_r, self.fwd_l):
            copy.wait_send()


def pre_kernel(
    ctx, wsh, hid, gain, router,
    normed_o, mixed_o, logits_o, routes_o,
    wg, part, r1, r2, sq, lg,
    lsem, xs, xr, zs, zr, ss, sr, ys, yr, qs, qr,
):
    e, z, x, c, y = coords()
    xr_, xl_ = lax.rem(x + 1, NX), lax.rem(x + NX - 1, NX)
    to_r, to_l = eid(z, xr_, c), eid(z, xl_, c)
    to_u, to_d = eid(lax.rem(z + 1, NZ), x, c), eid(lax.rem(z + NZ - 1, NZ), x, c)
    sib = eid(z, x, 1 - c)
    yu, yd, yo = lax.rem(y + 1, NY), lax.rem(y + NY - 1, NY), lax.rem(y + 2, NY)
    for t in (to_r, to_l, to_u, to_d, sib):
        greet(t, y)
    for t in (yu, yd, yo):
        greet(e, t)
    pl.semaphore_wait(pltpu.get_barrier_semaphore(), 8)

    own = blk(z, c, x)
    mine = pltpu.make_async_copy(wsh, wg.at[own], lsem)
    mine.start()
    gx = XGather(
        wsh, wg, own, blk(z, c, xl_), blk(z, c, xr_), blk(z, c, lax.rem(x + 2, NX)),
        16, xs, xr, to_r, to_l, y,
    )
    gx.start()
    mine.wait()
    gx.forward()
    gx.finish()

    def plane(p, cc, n=NX, off=0):
        return wg.at[pl.ds(p * (NX * NC) + cc * NX + off, n)]

    def up(t):
        p = lax.rem(z + NZ - t, NZ)
        r = plane(p, c) if t < 3 else plane(p, c, 2, 0)
        return send(r, r, zs.at[t], zr.at[t], to_u, y)

    def down(t):
        p = lax.rem(z + t, NZ)
        r = plane(p, c) if t < 3 else plane(p, c, 2, 2)
        return send(r, r, zs.at[4 + t], zr.at[4 + t], to_d, y)

    def got(t, d):
        p = lax.rem(z + NZ + d * (t + 1), NZ)
        base = 0 if d < 0 else 4
        r = plane(p, c) if t < 3 else plane(p, c, 2, 0 if d < 0 else 2)
        send(r, r, zs.at[base + t], zr.at[base + t], to_u, y).wait_recv()

    def across(k, p, cc):
        r = plane(p, cc)
        return send(r, r, ss.at[k], sr.at[k], sib, y)

    up(0).start()
    down(0).start()
    across(0, z, c).start()
    for t in range(3):
        got(t, -1)
        up(t + 1).start()
        got(t, 1)
        down(t + 1).start()
        across(2 * t + 1, lax.rem(z + NZ - t - 1, NZ), c).start()
        across(2 * t + 2, lax.rem(z + t + 1, NZ), c).start()
    got(3, -1)
    got(3, 1)
    across(7, lax.rem(z + 4, NZ), c).start()
    order = [0, -1, 1, -2, 2, -3, 3, 4]
    for k in range(NZ):
        across(k, lax.rem(z + NZ + order[k], NZ), 1 - c).wait_recv()

    def columns(d):
        blocks = []
        for zz in range(2):
            for xx in range(NX):
                for cc in range(NC):
                    blocks.append(wg[(2 * d + zz) * (NX * NC) + cc * NX + xx, :, :FEAT])
        return nt(ctx[...], jnp.concatenate(blocks, axis=0))

    part[yo] = columns(yo)
    hrows = ROWS // 2
    lo, hi = pl.ds(0, hrows), pl.ds(hrows, hrows)
    a_u = send(part.at[yo, lo], r1.at[0], ys.at[0], yr.at[0], e, yu)
    a_d = send(part.at[yo, hi], r1.at[1], ys.at[1], yr.at[1], e, yd)
    a_u.start()
    a_d.start()
    part[yu] = columns(yu)
    part[yd] = columns(yd)
    a_u.wait_recv()
    part[yu, lo] = part[yu, lo] + r1[0]
    b_u = send(part.at[yu], r2.at[0], ys.at[2], yr.at[2], e, yu)
    b_u.start()
    a_d.wait_recv()
    part[yd, hi] = part[yd, hi] + r1[1]
    b_d = send(part.at[yd], r2.at[1], ys.at[3], yr.at[3], e, yd)
    b_d.start()
    attn = columns(y)
    routes_o[...] = wg[:, 0:16, FEAT : FEAT + ROWS]
    b_u.wait_recv()
    b_d.wait_recv()
    mixed = hid[...].astype(F32) + (attn + r2[0] + r2[1])
    mixed_o[...] = mixed

    def spread(buf, base):
        copies = []
        for k, t in enumerate((yu, yd, yo)):
            copies.append(send(buf.at[3], buf.at[k], qs.at[base + k], qr.at[base + k], e, t))
        for copy in copies:
            copy.start()
        for copy in copies:
            copy.wait_recv()
        return copies

    sq[3] = jnp.broadcast_to(jnp.sum(mixed * mixed, axis=1, keepdims=True), (ROWS, 128))
    c1 = spread(sq, 0)
    squares = (sq[0] + sq[1]) + (sq[2] + sq[3])
    inverse = lax.rsqrt(squares[:, :1] / WIDTH + 1e-06)
    normed32 = mixed * inverse * gain[...]
    normed_o[...] = normed32.astype(BF16)
    lg[3] = jnp.dot(
        normed32, router[...], precision=lax.Precision.HIGHEST, preferred_element_type=F32
    )
    c2 = spread(lg, 3)
    logits_o[...] = (lg[0] + lg[1]) + (lg[2] + lg[3])

    gx.drain()
    for t in range(4):
        up(t).wait_send()
        down(t).wait_send()
    for k in range(NZ):
        across(k, lax.rem(z + NZ + order[k], NZ), c).wait_send()
    for copy in [a_u, a_d, b_u, b_d] + c1 + c2:
        copy.wait_send()


def pre(ctx, wsh, hid, gain, router):
    dma = pltpu.SemaphoreType.DMA
    vm = pl.BlockSpec(memory_space=pltpu.VMEM)
    return pl.pallas_call(
        pre_kernel,
        name="attention_norm_router",
        out_shape=[
            jax.ShapeDtypeStruct((ROWS, FEAT), BF16),
            jax.ShapeDtypeStruct((ROWS, FEAT), F32),
            jax.ShapeDtypeStruct((ROWS, 128), F32),
            jax.ShapeDtypeStruct((NE, 16, ROWS), BF16),
        ],
        in_specs=[vm] * 5,
        out_specs=[vm] * 4,
        scratch_shapes=[
            pltpu.VMEM((NE, 32, FEAT + ROWS), BF16),
            pltpu.VMEM((NY, ROWS, FEAT), F32),
            pltpu.VMEM((2, ROWS // 2, FEAT), F32),
            pltpu.VMEM((2, ROWS, FEAT), F32),
            pltpu.VMEM((4, ROWS, 128), F32),
            pltpu.VMEM((4, ROWS, 128), F32),
            dma,
            dma((4,)), dma((4,)),
            dma((8,)), dma((8,)),
            dma((8,)), dma((8,)),
            dma((4,)), dma((4,)),
            dma((6,)), dma((6,)),
        ],
        compiler_params=pltpu.CompilerParams(
            collective_id=0, has_side_effects=True, vmem_limit_bytes=VMEM_LIMIT
        ),
    )(ctx, wsh, hid, gain, router)


def tail_kernel(
    normed, routes, wsh, win, wout,
    res_o, shared_o,
    tok, slot, xg, pb, r1, r2, wb, wi, wo, sbuf, rbuf, acc,
    lsem, wsem, xs, xr, zs, zr, ss, sr, wzs, wzr, wxs, wxr, wss, wsr, gs, gr, ps, pr, os_, or_,
):
    e, z, x, c, y = coords()
    xr_, xl_ = lax.rem(x + 1, NX), lax.rem(x + NX - 1, NX)
    xo_ = lax.rem(x + 2, NX)
    to_r, to_l = eid(z, xr_, c), eid(z, xl_, c)
    to_u, to_d = eid(lax.rem(z + 1, NZ), x, c), eid(lax.rem(z + NZ - 1, NZ), x, c)
    sib = eid(z, x, 1 - c)
    yu, yd, yo = lax.rem(y + 1, NY), lax.rem(y + NY - 1, NY), lax.rem(y + 2, NY)
    lo, hi = pl.ds(0, HALF), pl.ds(HALF, HALF)

    def hello(k, carry):
        greet(lax.rem(e + k, NE), y)
        return carry

    lax.fori_loop(1, NE, hello, 0)
    greet(e, yu)
    greet(e, yd)
    pl.semaphore_wait(pltpu.get_barrier_semaphore(), NE + 1)

    own = blk(z, c, x)
    keep = pltpu.make_async_copy(normed, tok.at[own], lsem.at[0])
    keep.start()
    gx = XGather(
        normed, tok, own, blk(z, c, xl_), blk(z, c, xr_), blk(z, c, xo_),
        ROWS // 2, xs, xr, to_r, to_l, y,
    )
    gx.start()

    def wblk(zz, cc, xx):
        return cc * (NX * NZ) + xx * NZ + zz

    wown = pltpu.make_async_copy(wsh, wb.at[wblk(z, c, x)], lsem.at[1])
    wown.start()
    loads = [
        pltpu.make_async_copy(win.at[0], wi.at[0, pl.ds(0, QUARTER)], wsem.at[0]),
        pltpu.make_async_copy(win.at[1], wi.at[1, pl.ds(0, QUARTER)], wsem.at[1]),
        pltpu.make_async_copy(wout, wo.at[pl.ds(0, QUARTER)], wsem.at[2]),
    ]
    for load in loads:
        load.start()
    pad = pl.ds(QUARTER, QPAD - QUARTER)
    wi[0, pad] = jnp.zeros((QPAD - QUARTER, WIDTH), BF16)
    wi[1, pad] = jnp.zeros((QPAD - QUARTER, WIDTH), BF16)
    wo[pad] = jnp.zeros((QPAD - QUARTER, WIDTH), BF16)

    def mark(b, carry):
        named = (routes[b].astype(F32) == e.astype(F32)).astype(F32)
        slot[pl.ds(b, 1), :] = jnp.sum(named, axis=0, keepdims=True)
        return carry

    lax.fori_loop(0, NE, mark, 0)
    before = lax.broadcasted_iota(jnp.int32, (ROWS, ROWS), 0) < lax.broadcasted_iota(
        jnp.int32, (ROWS, ROWS), 1
    )
    named = slot[...]
    rank = jnp.dot(named.astype(BF16), before.astype(F32).astype(BF16), preferred_element_type=F32)
    slot[...] = jnp.where(named > 0.5, rank, -1000.0)

    keep.wait()
    gx.forward()
    gx.finish()

    def plane(p, cc, n=NX, off=0):
        return tok.at[pl.ds(p * (NX * NC) + cc * NX + off, n)]

    def whole_up(t):
        r = plane(lax.rem(z + NZ - t, NZ), c)
        return send(r, r, zs.at[t], zr.at[t], to_u, y)

    def whole_down(t):
        r = plane(lax.rem(z + t, NZ), c)
        return send(r, r, zs.at[4 + t], zr.at[4 + t], to_d, y)

    def half_up(p):
        r = plane(p, c, 2, 0)
        return send(r, r, zs.at[3], zr.at[3], to_u, y)

    def half_down(p):
        r = plane(p, c, 2, 2)
        return send(r, r, zs.at[7], zr.at[7], to_d, y)

    def across(k, p, cc):
        r = plane(p, cc)
        return send(r, r, ss.at[k], sr.at[k], sib, y)

    def plane_of(k):
        t = lax.div(k + 1, 2)
        return lax.rem(z + NZ + t * (1 - 2 * lax.rem(k, 2)), NZ)

    def stage_tokens(k):
        t = lax.div(k + 1, 2)
        p = plane_of(k)

        @pl.when(k == 0)
        def _():
            whole_up(0).start()
            whole_down(0).start()

        @pl.when((k > 0) & (k < 7) & (lax.rem(k, 2) == 1))
        def _():
            r = plane(p, c)
            send(r, r, zs.at[t - 1], zr.at[t - 1], to_u, y).wait_recv()

            @pl.when(t < 3)
            def _():
                whole_up(t).start()

            @pl.when(t == 3)
            def _():
                half_up(p).start()

        @pl.when((k > 0) & (lax.rem(k, 2) == 0))
        def _():
            r = plane(p, c)
            send(r, r, zs.at[3 + t], zr.at[3 + t], to_d, y).wait_recv()

            @pl.when(t < 3)
            def _():
                whole_down(t).start()

            @pl.when(t == 3)
            def _():
                half_down(p).start()

        @pl.when(k == 7)
        def _():
            half_up(p).wait_recv()
            half_down(p).wait_recv()

        across(k, p, c).start()

    def ag(i, k, who, rows, to):
        r = xg.at[i, who] if rows is None else xg.at[i, who, rows]
        return send(r, r, gs.at[k, i], gr.at[k, i], e, to)

    def stage_rows(i):
        @pl.when(i < NZ)
        def _():
            p = plane_of(i)
            across(i, p, 1 - c).wait_recv()
            rows = lax.broadcasted_iota(jnp.int32, (CHUNK, ROWS), 0).astype(F32)

            def pick(b, total):
                k = p * (NX * NC) + b
                where = slot[pl.ds(k, 1), :] + (CAP * b).astype(F32)
                onehot = (rows == where).astype(F32).astype(BF16)
                return total + jnp.dot(onehot, tok[k], preferred_element_type=F32)

            taken = lax.fori_loop(0, NX * NC, pick, jnp.zeros((CHUNK, FEAT), F32))
            xg[i, y] = taken.astype(BF16)

        @pl.when(i == NZ)
        def _():
            xg[i, y, pl.ds(0, ROWS)] = normed[...]
            xg[i, y, pl.ds(ROWS, CHUNK - ROWS)] = jnp.zeros((CHUNK - ROWS, FEAT), BF16)

        ag(i, 0, y, None, yu).start()
        ag(i, 1, y, None, yd).start()

    def stage_relay(i):
        ag(i, 0, yd, None, yu).wait_recv()
        ag(i, 2, yd, lo, yu).start()
        ag(i, 1, yu, None, yd).wait_recv()
        ag(i, 3, yu, hi, yd).start()

    def rs1(i, k):
        rows, to = (lo, yu) if k == 0 else (hi, yd)
        return send(pb.at[i, yo, rows], r1.at[i, k], ps.at[k, i], pr.at[k, i], e, to)

    def rs2(i, k):
        to = yu if k == 0 else yd
        return send(pb.at[i, to], r2.at[i, k], ps.at[2 + k, i], pr.at[2 + k, i], e, to)

    def gated(gate, value):
        return (gate / (1.0 + jnp.exp(-gate)) * value).astype(BF16)

    def stage_experts(i):
        ag(i, 2, yo, lo, yu).wait_recv()
        ag(i, 3, yo, hi, yd).wait_recv()

        @pl.when(i < NZ)
        def _():
            both = []
            for h in range(2):
                total = jnp.zeros((CHUNK, QPAD), F32)
                for k in range(NY):
                    total = total + nt(xg[i, k], wi[h, :, k * FEAT : (k + 1) * FEAT])
                both.append(total)
            hidden = gated(both[0], both[1])

            def down(d, carry):
                w = wo[:, pl.ds(pl.multiple_of(d * FEAT, FEAT), FEAT)]
                pb[i, d] = jnp.dot(hidden, w, preferred_element_type=F32).astype(BF16)
                return carry

            lax.fori_loop(0, NY, down, 0)

        @pl.when(i == NZ)
        def _():
            for k in range(NX):
                column = wb.at[pl.ds((1 - c) * (NX * NZ) + k * NZ, NZ)]
                send(column, column, wss.at[k], wsr.at[k], sib, y).wait_recv()
            acc[...] = jnp.zeros((CHUNK, 2 * SPAD), F32)

            def into(zz, carry):
                w = jnp.concatenate(
                    [wb[wblk(zz, cc, xx), :, : 2 * SPAD] for xx in range(NX) for cc in range(NC)],
                    axis=0,
                )
                off = pl.multiple_of(lax.rem(zz, 2) * 256, 256)
                acc[...] += jnp.dot(
                    xg[i, lax.div(zz, 2), :, pl.ds(off, 256)], w, preferred_element_type=F32
                )
                return carry

            lax.fori_loop(0, NZ, into, 0)
            hidden = gated(acc[:, :SPAD], acc[:, SPAD:])

            def out(d, carry):
                w = jnp.concatenate(
                    [
                        wb[wblk(2 * d + zz, cc, xx), :, 2 * SPAD :]
                        for zz in range(2)
                        for xx in range(NX)
                        for cc in range(NC)
                    ],
                    axis=0,
                )
                pb[i, d] = nt(hidden, w).astype(BF16)
                return carry

            lax.fori_loop(0, NY, out, 0)

        rs1(i, 0).start()
        rs1(i, 1).start()

    def stage_reduce(i):
        rs1(i, 0).wait_recv()
        pb[i, yu, lo] = (pb[i, yu, lo].astype(F32) + r1[i, 0].astype(F32)).astype(BF16)
        rs2(i, 0).start()
        rs1(i, 1).wait_recv()
        pb[i, yd, hi] = (pb[i, yd, hi].astype(F32) + r1[i, 1].astype(F32)).astype(BF16)
        rs2(i, 1).start()

    def dest(i, b):
        return eid(plane_of(i), lax.rem(b, NX), lax.div(b, NX))

    def back(i, b):
        to = dest(i, b)
        return to, send(sbuf.at[i, b], rbuf.at[e], os_.at[i * (NX * NC) + b], or_.at[e], to, y)

    def stage_return(i):
        rs2(i, 0).wait_recv()
        rs2(i, 1).wait_recv()
        total = pb[i, y].astype(F32) + r2[i, 0].astype(F32) + r2[i, 1].astype(F32)

        @pl.when(i < NZ)
        def _():
            to_row = lax.broadcasted_iota(jnp.int32, (NX * NC * SLOT, CHUNK), 0)
            of_row = lax.broadcasted_iota(jnp.int32, (NX * NC * SLOT, CHUNK), 1)
            inner = of_row - CAP * lax.shift_right_logical(to_row, 5)
            move = (inner == (to_row & (SLOT - 1))) & (inner < CAP) & (inner >= 0)
            spaced = jnp.dot(
                move.astype(F32).astype(BF16), total.astype(BF16), preferred_element_type=F32
            )
            sbuf[i] = spaced.astype(BF16).reshape(NX * NC, SLOT, FEAT)

            def go(b, carry):
                to, copy = back(i, b)

                @pl.when(to != e)
                def _():
                    copy.start()

                @pl.when(to == e)
                def _():
                    rbuf[e] = sbuf[i, b]

                return carry

            lax.fori_loop(0, NX * NC, go, 0)

        @pl.when(i == NZ)
        def _():
            shared_o[...] = total[:ROWS]

    def wz(t, d, half):
        p = lax.rem(z + NZ - d * t, NZ)
        r = wb.at[wblk(p, c, x)]
        if half:
            r = wb.at[wblk(p, c, x), pl.ds(0 if d > 0 else 16, 16)]
        k = (0 if d > 0 else 4) + t
        return send(r, r, wzs.at[k], wzr.at[k], to_u if d > 0 else to_d, y)

    def wz_got(t, d, half):
        p = lax.rem(z + NZ - d * (t + 1), NZ)
        r = wb.at[wblk(p, c, x)]
        if half:
            r = wb.at[wblk(p, c, x), pl.ds(0 if d > 0 else 16, 16)]
        k = (0 if d > 0 else 4) + t
        send(r, r, wzs.at[k], wzr.at[k], to_u if d > 0 else to_d, y).wait_recv()

    def col(xx, n=NZ, off=0):
        return wb.at[pl.ds(c * (NX * NZ) + xx * NZ + off, n)]

    def wx(k):
        r, to = [
            (col(x), to_r), (col(x), to_l), (col(xl_, 4, 0), to_r), (col(xr_, 4, 4), to_l)
        ][k]
        return send(r, r, wxs.at[k], wxr.at[k], to, y)

    def wx_got(k):
        r = [col(xl_), col(xr_), col(xo_, 4, 0), col(xo_, 4, 4)][k]
        send(r, r, wxs.at[k], wxr.at[k], to_r, y).wait_recv()

    def wsib(xx):
        r = col(xx)
        return send(r, r, wss.at[xx], wsr.at[xx], sib, y)

    def stage_weights(j):
        @pl.when(j == 0)
        def _():
            wown.wait()
            wz(0, 1, False).start()
            wz(0, -1, False).start()

        for t in range(3):

            @pl.when(j == t + 1)
            def _(t=t):
                wz_got(t, 1, False)
                wz(t + 1, 1, t == 2).start()
                wz_got(t, -1, False)
                wz(t + 1, -1, t == 2).start()

        @pl.when(j == 4)
        def _():
            wz_got(3, 1, True)
            wz_got(3, -1, True)
            wx(0).start()
            wx(1).start()
            wsib(x).start()

        @pl.when(j == 7)
        def _():
            wx_got(0)
            wx(2).start()
            wx_got(1)
            wx(3).start()
            wsib(xl_).start()
            wsib(xr_).start()

        @pl.when(j == 10)
        def _():
            wx_got(2)
            wx_got(3)
            wsib(xo_).start()

    stage_tokens(jnp.int32(0))

    def step(j, carry):
        @pl.when(j + 1 < NZ)
        def _():
            stage_tokens(j + 1)

        @pl.when(j < NCH)
        def _():
            stage_rows(j)

        stage_weights(j)

        @pl.when((j >= 1) & (j < NCH + 1))
        def _():
            stage_relay(j - 1)

        @pl.when(j == 2)
        def _():
            for load in loads:
                load.wait()

        @pl.when((j >= 2) & (j < NCH + 2))
        def _():
            stage_experts(j - 2)

        @pl.when((j >= 3) & (j < NCH + 3))
        def _():
            stage_reduce(j - 3)

        @pl.when(j >= 4)
        def _():
            stage_return(j - 4)

        return carry

    lax.fori_loop(0, NCH + 4, step, 0)

    def arrive(k, carry):
        s = lax.rem(e + k, NE)
        send(rbuf.at[s], rbuf.at[s], os_.at[0], or_.at[s], sib, y).wait_recv()
        return carry

    lax.fori_loop(1, NE, arrive, 0)
    res_o[...] = rbuf[...]

    gx.drain()
    for t in range(3):
        whole_up(t).wait_send()
        whole_down(t).wait_send()
    half_up(lax.rem(z + NZ - 3, NZ)).wait_send()
    half_down(lax.rem(z + 3, NZ)).wait_send()
    for t in range(4):
        wz(t, 1, t == 3).wait_send()
        wz(t, -1, t == 3).wait_send()
        wx(t).wait_send()
        wsib(t).wait_send()

    def drain(i, carry):
        @pl.when(i < NZ)
        def _():
            across(i, plane_of(i), c).wait_send()

            def sent(b, inner):
                to, copy = back(i, b)

                @pl.when(to != e)
                def _():
                    copy.wait_send()

                return inner

            lax.fori_loop(0, NX * NC, sent, 0)

        ag(i, 0, y, None, yu).wait_send()
        ag(i, 1, y, None, yd).wait_send()
        ag(i, 2, yd, lo, yu).wait_send()
        ag(i, 3, yu, hi, yd).wait_send()
        for k in range(2):
            rs1(i, k).wait_send()
            rs2(i, k).wait_send()
        return carry

    lax.fori_loop(0, NCH, drain, 0)


def tail(normed, routes, wsh, win, wout):
    dma = pltpu.SemaphoreType.DMA
    vm = pl.BlockSpec(memory_space=pltpu.VMEM)
    hbm = pl.BlockSpec(memory_space=pl.ANY)
    return pl.pallas_call(
        tail_kernel,
        name="routed_and_shared_experts",
        out_shape=[
            jax.ShapeDtypeStruct((NE, SLOT, FEAT), BF16),
            jax.ShapeDtypeStruct((ROWS, FEAT), F32),
        ],
        in_specs=[vm, vm, vm, hbm, hbm],
        out_specs=[vm] * 2,
        scratch_shapes=[
            pltpu.VMEM((NE, ROWS, FEAT), BF16),
            pltpu.VMEM((NE, ROWS), F32),
            pltpu.VMEM((NCH, NY, CHUNK, FEAT), BF16),
            pltpu.VMEM((NCH, NY, CHUNK, FEAT), BF16),
            pltpu.VMEM((NCH, 2, HALF, FEAT), BF16),
            pltpu.VMEM((NCH, 2, CHUNK, FEAT), BF16),
            pltpu.VMEM((NE, 32, 3 * SPAD), BF16),
            pltpu.VMEM((2, QPAD, WIDTH), BF16),
            pltpu.VMEM((QPAD, WIDTH), BF16),
            pltpu.VMEM((NZ, NX * NC, SLOT, FEAT), BF16),
            pltpu.VMEM((NE, SLOT, FEAT), BF16),
            pltpu.VMEM((CHUNK, 2 * SPAD), F32),
            dma((2,)), dma((3,)),
            dma((4,)), dma((4,)),
            dma((8,)), dma((8,)),
            dma((8,)), dma((8,)),
            dma((8,)), dma((8,)),
            dma((4,)), dma((4,)),
            dma((4,)), dma((4,)),
            dma((4, NCH)), dma((4, NCH)),
            dma((4, NCH)), dma((4, NCH)),
            dma((NE,)), dma((NE,)),
        ],
        compiler_params=pltpu.CompilerParams(
            collective_id=1, has_side_effects=True, vmem_limit_bytes=VMEM_LIMIT
        ),
    )(normed, routes, wsh, win, wout)


def combine(logits, route_ids, res):
    ids = jnp.arange(NE, dtype=jnp.int32)
    chosen = jnp.any(route_ids[:, :, None] == ids[None, None, :], axis=1)
    masked = jnp.where(chosen, logits, -jnp.inf)
    weight = jnp.where(chosen, jnp.exp(logits - jnp.max(masked, axis=1, keepdims=True)), 0.0)
    gates = weight / jnp.sum(weight, axis=1, keepdims=True)
    rows = jnp.arange(ROWS, dtype=jnp.int32)
    before = (rows[None, :] < rows[:, None]).astype(BF16)
    rank = jnp.dot(before, chosen.astype(BF16), preferred_element_type=F32)
    lane = jnp.arange(NE * SLOT, dtype=jnp.int32)
    expand = (ids[:, None] == lane[None, :] // SLOT).astype(BF16)
    high = lax.reduce_precision(gates, 8, 7)
    low = gates - high
    stacked = jnp.concatenate(
        [jnp.where(chosen, rank, 255.0).astype(BF16), high.astype(BF16), low.astype(BF16)], axis=0
    )
    wide = jnp.dot(stacked, expand, preferred_element_type=F32).reshape(3, ROWS, NE * SLOT)
    here = wide[0] == (lane % SLOT).astype(F32)[None, :]
    table = jnp.where(here[None], wide[1:], 0.0).astype(BF16)
    out = jnp.dot(
        table.reshape(2 * ROWS, NE * SLOT),
        res.reshape(NE * SLOT, FEAT),
        preferred_element_type=F32,
    )
    return out[:ROWS] + out[ROWS:]


def per_device(
    hidden_state, context, out_proj, norm_gain, router_weight,
    expert_in, expert_out, shared_in, shared_out, route_ids,
):
    ids = jnp.pad(
        route_ids.T.astype(BF16), ((0, 32 - TOP), (0, 0)), constant_values=-1.0
    )
    wsh = jnp.concatenate([out_proj.T, ids], axis=1)
    router = jnp.pad(router_weight, ((0, 0), (0, 128 - NE)))
    gain = norm_gain.astype(F32)[None, :]
    normed, mixed, logits, routes = pre(context, wsh, hidden_state, gain, router)
    gap = ((0, 0), (0, 0), (0, SPAD - SWIDTH))
    shard = jnp.concatenate(
        [
            jnp.pad(shared_in, gap).reshape(32, 2 * SPAD),
            jnp.pad(shared_out.T, ((0, 0), (0, SPAD - SWIDTH))),
        ],
        axis=1,
    )
    win = jnp.transpose(expert_in[0], (1, 2, 0))
    res, shared = tail(normed, routes, shard, win, expert_out[0])
    return mixed + combine(logits[:, :NE], route_ids, res) + shared


def solution(mesh):
    return jax.shard_map(
        per_device,
        mesh=mesh,
        in_specs=(
            P("expert", "mp"),
            P("expert", "mp"),
            P("mp", "expert"),
            P("mp"),
            P("mp", None),
            P("expert", None, None, "mp"),
            P("expert", "mp", None),
            P("expert", None, "mp"),
            P("mp", "expert"),
            P("expert", None),
        ),
        out_specs=P("expert", "mp"),
        check_vma=False,
    )
```

time: 549 us -> 247 us (0.45)
  waiting for transfers between devices: 326 us -> 0 us
  Pallas kernels: 0 us -> 232 us
  blocking collectives: 82.6 us -> 0 us
  local copies, waits for them, and re-layouts: 78.1 us -> 1.97 us
  matrix products: 23.6 us -> 3.37 us
  between operations: 13.8 us -> 0.16 us
  starting transfers between devices: 11.2 us -> 0 us
    pallas_call x0 -> x2, Pallas kernels: none -> 232 us  [the longest x1 170 us: tail(): pl.pallas_call(tail_kernel, name='routed_and_shared_experts', out_shape=[...]
    all_to_all x1 -> x0, waiting for transfers between devices: 158 us -> none  [per_device(): lax.all_to_all(partial_out, 'expert', split_axis=0, concat_axis=0, tiled=...]
    all_gather x4 -> x0, waiting for transfers between devices: 147 us -> none  [the longest x1 84.3 us: per_device(): lax.all_gather(out_proj, 'expert', axis=1, tiled=True)]
    all_to_all x1 -> x0, blocking collectives: 52.8 us -> none  [per_device(): lax.all_to_all(outgoing, 'expert', split_axis=0, concat_axis=0, tiled=True)]
    reshape x4 -> x0, local copies, waits for them, and re-layouts: 29.5 us -> none  [the longest x1 8.99 us: per_device(): lax.all_gather(incoming, 'mp', axis=2, tiled=True)]
    gather x8 -> x0, local copies, waits for them, and re-layouts: 23.8 us -> none  [the longest x1 10.3 us: per_device(): picked = result.reshape(experts * capacity, result.shape[2])[slot_of]]
    dot_general x6 -> x3, matrix products: 23.6 us -> 3.37 us  [the longest x1 2.66 us: combine(): jnp.dot(table.reshape(2 * ROWS, NE * SLOT), res.reshape(NE * SLOT, FEAT),...]
    psum x2 -> x0, blocking collectives: 19.1 us -> none  [the longest x1 12.5 us: per_device(): lax.psum(jnp.dot(normed32, router_weight, precision=lax.Precision.HIGHEST...]
  transfers between devices with their start and end apart: 8 -> 0, of which waited for: 5 -> 0; matrix products, arithmetic and copies ran while one was open for 17% -> 0% of each run, Pallas kernels for 0% -> 0%
where the time goes in v1:
time: 247 us
  Pallas kernels  232 us (94%)
  other arithmetic  9.89 us (4%)
  matrix products  3.37 us (1%)
    pallas_call x1, Pallas kernels, tail(): pl.pallas_call(tail_kernel, name='routed_and_shared_experts', out_shape=[...  170 us
    pallas_call x1, Pallas kernels, pre(): pl.pallas_call(pre_kernel, name='attention_norm_router', out_shape=[jax.S...  61.5 us

profile of v1, /device:TPU:1, one launch (start us, length us, event | category | flops | bytes accessed | tf_op | source)
XLA Modules:
  0.0 247.0 jit_solution(7147964462437281663)
XLA Ops:
  0.0 1.0 copy.13
  1.0 0.7 pad.17.router
  1.8 0.7 convert_bitcast_fusion
  2.5 1.4 fusion.18.wsh
  3.8 1.3 broadcast_in_dim.47
  5.1 61.5 %attention_norm_router.1 = (bf16[128,512]{1,0:T(8,128)(2,1)}, f32[128,512]{1,0:T(8,128)}, f32[128,128]{1,0:T(8,128)}, bf16[64,16,128]{2,1,0:T(8,128)(2,1)}) custom-call(bf16[128,512]{1,0:T(8,128)(2,1)} %ctx.1, bf16[32,640]{1,0:T(8,128)(2,1)} %fusion.18.wsh, bf16[128,512]{1,0:T(8,128)(2,1)} %hid.1, f32[1,512]{1,0:T(1,128)} %bitcast.23, f32[512,128]{1,0:T(8,128)} %pad.17.router), custom_call_target="tpu_custom_call" | custom-call | tf_op jit(solution)/shard_map/attention_norm_router/pallas_call | solution.py:230
  66.6 0.7 fusion.7
  67.3 0.1 copy.14
  67.4 0.9 select_reduce_fusion
  68.4 1.0 fusion.17
  69.4 1.0 reduce-precision_convert_fusion
  70.4 0.1 fusion.1
  70.5 0.6 fusion.2
  71.1 0.0 copy-start.2
  71.1 0.0 copy-start.3
  71.1 0.2 slice_compare_fusion
  71.3 1.3 fusion
  72.6 0.0 copy-done.2
  72.6 0.1 pad.18
  72.7 0.0 copy-done.3
  72.7 0.7 fusion.8.wsh
  73.4 170.1 %routed_and_shared_experts.1 = (bf16[64,32,512]{2,1,0:T(8,128)(2,1)}, f32[128,512]{1,0:T(8,128)}) custom-call(bf16[128,512]{1,0:T(8,128)(2,1)} %get-tuple-element.13.normed, bf16[64,16,128]{2,1,0:T(8,128)(2,1)} %get-tuple-element.14.routes, bf16[32,2304]{1,0:T(8,128)(2,1)} %fusion.8.wsh, bf16[2,352,2048]{2,1,0:T(8,128)(2,1)} %bitcast.17, ...), custom_call_target="tpu_custom_call" | custom-call | tf_op jit(solution)/shard_map/routed_and_shared_experts/pallas_call | solution.py:714
  243.5 2.7 %fusion.29 = f32[256,512]{1,0:T(8,128)S(1)} fusion(bf16[256,2048]{1,0:T(8,128)(2,1)} %fusion, bf16[2048,512]{1,0:T(8,128)(2,1)} %bitcast.24), kind=kOutput, calls=%fused_computation.46 | convolution fusion | flops 536870912 | bytes 3670016 | tf_op jit(solution)/shard_map/dot_general | solution.py:772
  246.2 0.8 fusion.5
  (8 shorter events, 0.0 us)
Async XLA Ops:
  71.1 1.5 copy-start.2
  71.1 1.6 copy-start.3
  243.5 2.7 %copy-start = (f32[128,512]{1,0:T(8,128)S(1)}, f32[128,512]{1,0:T(8,128)}, u32[]{:S(2)}) copy-start(f32[128,512]{1,0:T(8,128)} %get-tuple-element.11) | copy-start | bytes 786436
  243.5 2.7 %copy-start.1 = (f32[128,512]{1,0:T(8,128)S(1)}, f32[128,512]{1,0:T(8,128)}, u32[]{:S(2)}) copy-start(f32[128,512]{1,0:T(8,128)} %get-tuple-element.16) | copy-start | bytes 786436

commit v2 on v0

v2 whole, which is shorter than its diff:
```python
import jax
import jax.numpy as jnp
from jax import lax
from jax.experimental import pallas as pl
from jax.experimental.pallas import tpu as pltpu
from jax.sharding import PartitionSpec as P

NZ, NX, NC, NY = 8, 4, 2, 4
NE = NZ * NX * NC
ROWS, FEAT, WIDTH = 128, 512, 2048
TOP, CAP, PACK, PWIDTH = 6, 20, 16, 640
QUARTER, QPAD = 352, 384
SWIDTH, SPAD = 704, 768
CHUNK = NX * NC * CAP
HALF = CHUNK // 2
NCH = NZ + 1
SHARED_AT = 7
ORDER = sum(d << (3 * k) for k, d in enumerate((0, 7, 1, 6, 5, 4, 3, 2)))
F32, BF16 = jnp.float32, jnp.bfloat16
VMEM_LIMIT = 64 * 1024 * 1024 - 65536


def coords():
    e = lax.axis_index("expert")
    y = lax.axis_index("mp")
    z = lax.div(e, NX * NC)
    x = lax.rem(lax.div(e, NC), NX)
    c = lax.rem(e, NC)
    return e, z, x, c, y


def eid(z, x, c):
    return z * (NX * NC) + x * NC + c


def blk(z, c, x):
    return z * (NX * NC) + c * NX + x


def send(src, dst, ssem, rsem, e, y):
    return pltpu.make_async_remote_copy(
        src_ref=src,
        dst_ref=dst,
        send_sem=ssem,
        recv_sem=rsem,
        device_id={"expert": e, "mp": y},
        device_id_type=pl.DeviceIdType.MESH,
    )


def greet(e, y):
    pl.semaphore_signal(
        pltpu.get_barrier_semaphore(),
        inc=1,
        device_id={"expert": e, "mp": y},
        device_id_type=pl.DeviceIdType.MESH,
    )


def nt(a, b):
    return lax.dot_general(a, b, (((1,), (1,)), ((), ())), preferred_element_type=F32)


def mixer_kernel(
    ctx, opt, ids, hid, gain, router, wsh, win, wout,
    out,
    wga, wgb, part, p1, p2, sq, lg, mixed, shared, tab,
    tok, slot, xg, pb, r1, r2, wb, wi, wo, sbuf, rbuf, acc,
    wsem,
    axs, axr, azs, azr, ass, asr, bzs, bzr, bxs, bxr, bss, bsr,
    ys, yr, qs, qr,
    xs, xr, z0s, z0r, zs, zr, ss, sr,
    wzs, wzr, wxs, wxr, wss, wsr,
    gs, gr, ps, pr, os_, or_,
):
    e, z, x, c, y = coords()
    xr_, xl_, xo_ = lax.rem(x + 1, NX), lax.rem(x + NX - 1, NX), lax.rem(x + 2, NX)
    to_r, to_l = eid(z, xr_, c), eid(z, xl_, c)
    to_u, to_d = eid(lax.rem(z + 1, NZ), x, c), eid(lax.rem(z + NZ - 1, NZ), x, c)
    sib = eid(z, x, 1 - c)
    yu, yd, yo = lax.rem(y + 1, NY), lax.rem(y + NY - 1, NY), lax.rem(y + 2, NY)
    lo, hi = pl.ds(0, HALF), pl.ds(HALF, HALF)
    far = lax.rem(z + 4, NZ)

    def zat(d):
        return lax.rem(z + NZ + d, NZ)

    def hello(k, carry):
        greet(lax.rem(e + k, NE), y)
        return carry

    lax.fori_loop(1, NE, hello, 0)
    for t in (yu, yd, yo):
        greet(e, t)

    loads = [
        pltpu.make_async_copy(win.at[0], wi.at[0, pl.ds(0, QUARTER)], wsem.at[0]),
        pltpu.make_async_copy(win.at[1], wi.at[1, pl.ds(0, QUARTER)], wsem.at[1]),
        pltpu.make_async_copy(wout, wo.at[pl.ds(0, QUARTER)], wsem.at[2]),
    ]
    for load in loads:
        load.start()

    def wblk(zz, cc, xx):
        return cc * (NX * NZ) + xx * NZ + zz

    own, wown = blk(z, c, x), wblk(z, c, x)
    names = jnp.concatenate(
        [ids[...].astype(F32), jnp.full((ROWS - TOP, ROWS), -1.0, F32)], axis=0
    )
    wga[own, :, pl.ds(0, FEAT)] = opt[0:16, :]
    wga[own, :, pl.ds(FEAT, ROWS)] = names[:16].astype(BF16)
    wgb[wown] = opt[16:32, :]
    wb[wown] = wsh[...]
    pl.semaphore_wait(pltpu.get_barrier_semaphore(), NE + 2)

    def ax(k):
        b, to = [(own, to_r), (own, to_l), (blk(z, c, xl_), to_r)][k]
        return send(wga.at[b], wga.at[b], axs.at[k], axr.at[k], to, y)

    def ax_got(k):
        b = blk(z, c, [xl_, xr_, xo_][k])
        send(wga.at[b], wga.at[b], axs.at[k], axr.at[k], to_r, y).wait_recv()

    def a_plane(p, cc, n=NX, off=0):
        return wga.at[pl.ds(p * (NX * NC) + cc * NX + off, n)]

    def az(t, d):
        p = zat(-d * t)
        r = a_plane(p, c) if t < 3 else a_plane(p, c, 2, 0 if d > 0 else 2)
        k = t if d > 0 else 4 + t
        return send(r, r, azs.at[k], azr.at[k], to_u if d > 0 else to_d, y)

    def az_got(t, d):
        p = zat(-d * (t + 1))
        r = a_plane(p, c) if t < 3 else a_plane(p, c, 2, 0 if d > 0 else 2)
        k = t if d > 0 else 4 + t
        send(r, r, azs.at[k], azr.at[k], to_u, y).wait_recv()

    def a_sib(d, cc):
        r = a_plane(zat(d), cc)
        return send(r, r, ass.at[d % NZ], asr.at[d % NZ], sib, y)

    def bz(t, d):
        r = wgb.at[wblk(zat(-d * t), c, x)]
        k = t if d > 0 else 4 + t
        return send(r, r, bzs.at[k], bzr.at[k], to_u if d > 0 else to_d, y)

    def bz_got(t, d):
        r = wgb.at[wblk(zat(-d * (t + 1)), c, x)]
        k = t if d > 0 else 4 + t
        send(r, r, bzs.at[k], bzr.at[k], to_u, y).wait_recv()

    def b_col(xx, cc, n=NZ, off=0):
        return wgb.at[pl.ds(cc * (NX * NZ) + xx * NZ + off, n)]

    def bx(k):
        r, to = [
            (b_col(x, c), to_r), (b_col(x, c), to_l),
            (b_col(xl_, c, 4, 0), to_r), (b_col(xr_, c, 4, 4), to_l),
        ][k]
        return send(r, r, bxs.at[k], bxr.at[k], to, y)

    def bx_got(k):
        r = [b_col(xl_, c), b_col(xr_, c), b_col(xo_, c, 4, 0), b_col(xo_, c, 4, 4)][k]
        send(r, r, bxs.at[k], bxr.at[k], to_r, y).wait_recv()

    xoff = (x, xr_, xo_, xl_)

    def b_sib(k, cc):
        r = b_col(xoff[k], cc)
        return send(r, r, bss.at[k], bsr.at[k], sib, y)

    ax(0).start()
    ax(1).start()
    bz(0, 1).start()
    bz(0, -1).start()
    ax_got(0)
    ax(2).start()
    ax_got(1)
    bz_got(0, 1)
    bz(1, 1).start()
    bz_got(0, -1)
    bz(1, -1).start()
    ax_got(2)
    az(0, 1).start()
    az(0, -1).start()
    a_sib(0, c).start()
    bz_got(1, 1)
    bz(2, 1).start()
    bz_got(1, -1)
    bz(2, -1).start()
    az_got(0, 1)
    az(1, 1).start()
    az_got(0, -1)
    az(1, -1).start()
    a_sib(-1, c).start()
    a_sib(1, c).start()
    bz_got(2, 1)
    bz(3, 1).start()
    bz_got(2, -1)
    az_got(1, 1)
    az(2, 1).start()
    az_got(1, -1)
    az(2, -1).start()
    bz_got(3, 1)
    bx(0).start()
    bx(1).start()
    a_sib(-2, c).start()
    a_sib(2, c).start()
    b_sib(0, c).start()
    az_got(2, 1)
    az(3, 1).start()
    az_got(2, -1)
    az(3, -1).start()
    a_sib(-3, c).start()
    a_sib(3, c).start()
    bx_got(0)
    bx(2).start()
    bx_got(1)
    bx(3).start()
    b_sib(3, c).start()
    b_sib(1, c).start()
    az_got(3, 1)
    az_got(3, -1)
    a_sib(4, c).start()
    bx_got(2)
    bx_got(3)
    b_sib(2, c).start()

    def wz(t, d):
        r = wb.at[wblk(zat(-d * t), c, x)]
        if t == 3:
            r = wb.at[wblk(zat(-d * t), c, x), pl.ds(0 if d > 0 else 16, 16)]
        k = t if d > 0 else 4 + t
        return send(r, r, wzs.at[k], wzr.at[k], to_u if d > 0 else to_d, y)

    def wz_got(t, d):
        r = wb.at[wblk(zat(-d * (t + 1)), c, x)]
        if t == 3:
            r = wb.at[wblk(zat(-d * (t + 1)), c, x), pl.ds(0 if d > 0 else 16, 16)]
        k = t if d > 0 else 4 + t
        send(r, r, wzs.at[k], wzr.at[k], to_u, y).wait_recv()

    def wz_step(t):
        for d in (1, -1):
            wz_got(t - 1, d)
            wz(t, d).start()

    def col(xx, cc, n=NZ, off=0):
        return wb.at[pl.ds(cc * (NX * NZ) + xx * NZ + off, n)]

    def wx(k):
        r, to = [
            (col(x, c), to_r), (col(x, c), to_l),
            (col(xl_, c, 4, 0), to_r), (col(xr_, c, 4, 4), to_l),
        ][k]
        return send(r, r, wxs.at[k], wxr.at[k], to, y)

    def wx_got(k):
        r = [col(xl_, c), col(xr_, c), col(xo_, c, 4, 0), col(xo_, c, 4, 4)][k]
        send(r, r, wxs.at[k], wxr.at[k], to_r, y).wait_recv()

    def wsib(k, cc):
        r = col(xoff[k], cc)
        return send(r, r, wss.at[k], wsr.at[k], sib, y)

    wz(0, 1).start()
    wz(0, -1).start()
    for d in (0, -1, 1, -2, 2, -3, 3, 4):
        a_sib(d, 1 - c).wait_recv()
    for k in range(NX):
        b_sib(k, 1 - c).wait_recv()

    def columns(d):
        blocks = []
        for zz in range(2):
            for xx in range(NX):
                for cc in range(NC):
                    p = 2 * d + zz
                    blocks.append(wga[blk(p, cc, xx), :, pl.ds(0, FEAT)])
                    blocks.append(wgb[wblk(p, cc, xx)])
        return nt(ctx[...], jnp.concatenate(blocks, axis=0))

    hrows = ROWS // 2
    plo, phi = pl.ds(0, hrows), pl.ds(hrows, hrows)

    def pa(k):
        rows, to = [(plo, yu), (phi, yd)][k]
        return send(part.at[yo, rows], p1.at[k], ys.at[k], yr.at[k], e, to)

    def pb2(k):
        to = [yu, yd][k]
        return send(part.at[to], p2.at[k], ys.at[2 + k], yr.at[2 + k], e, to)

    part[yo] = columns(yo)
    pa(0).start()
    pa(1).start()
    part[yu] = columns(yu)
    part[yd] = columns(yd)
    pa(0).wait_recv()
    part[yu, plo] = part[yu, plo] + p1[0]
    pb2(0).start()
    pa(1).wait_recv()
    part[yd, phi] = part[yd, phi] + p1[1]
    pb2(1).start()
    part[y] = columns(y)
    wz_step(1)

    def mark(b, carry):
        same = (wga[b, :, pl.ds(FEAT, ROWS)].astype(F32) == e.astype(F32)).astype(F32)
        slot[pl.ds(b, 1), :] = jnp.sum(same, axis=0, keepdims=True)
        return carry

    lax.fori_loop(0, NE, mark, 0)
    r_i = lax.broadcasted_iota(jnp.int32, (ROWS, ROWS), 0)
    c_i = lax.broadcasted_iota(jnp.int32, (ROWS, ROWS), 1)
    named = slot[...]
    rank = jnp.dot(
        named.astype(BF16), (r_i < c_i).astype(F32).astype(BF16), preferred_element_type=F32
    )
    slot[...] = jnp.where(named > 0.5, rank, -1000.0)
    gap = pl.ds(QUARTER, QPAD - QUARTER)
    wi[0, gap] = jnp.zeros((QPAD - QUARTER, WIDTH), BF16)
    wi[1, gap] = jnp.zeros((QPAD - QUARTER, WIDTH), BF16)
    wo[gap] = jnp.zeros((QPAD - QUARTER, WIDTH), BF16)
    xg[NZ, y, pl.ds(ROWS, CHUNK - ROWS)] = jnp.zeros((CHUNK - ROWS, FEAT), BF16)

    pb2(0).wait_recv()
    pb2(1).wait_recv()
    mix = hid[...].astype(F32) + (part[y] + p2[0] + p2[1])
    mixed[...] = mix

    def spread(buf, base, k):
        return send(
            buf.at[3], buf.at[k], qs.at[base + k], qr.at[base + k], e, (yu, yd, yo)[k]
        )

    sums = jnp.broadcast_to(jnp.sum(mix * mix, axis=1, keepdims=True), (ROWS, ROWS))
    sq[3] = jnp.transpose(sums)[:8]
    for k in range(3):
        spread(sq, 0, k).start()
    wz_step(2)
    for k in range(3):
        spread(sq, 0, k).wait_recv()
    inverse = lax.rsqrt(((sq[0] + sq[1]) + (sq[2] + sq[3])) / WIDTH + 1e-06)
    inverse = jnp.transpose(jnp.broadcast_to(inverse[:1], (ROWS, ROWS)))[:, :1]
    normed32 = mix * inverse * gain[...].astype(F32)
    tok[own] = normed32.astype(BF16)
    xg[NZ, y, pl.ds(0, ROWS)] = normed32.astype(BF16)

    def tx(k):
        half = ROWS // 2
        r, to = [
            (tok.at[own], to_r), (tok.at[own], to_l),
            (tok.at[blk(z, c, xl_), pl.ds(0, half)], to_r),
            (tok.at[blk(z, c, xr_), pl.ds(half, half)], to_l),
        ][k]
        return send(r, r, xs.at[k], xr.at[k], to, y)

    def tx_got(k):
        half = ROWS // 2
        r = [
            tok.at[blk(z, c, xl_)], tok.at[blk(z, c, xr_)],
            tok.at[blk(z, c, xo_), pl.ds(0, half)], tok.at[blk(z, c, xo_), pl.ds(half, half)],
        ][k]
        send(r, r, xs.at[k], xr.at[k], to_r, y).wait_recv()

    def tz0(k, d):
        r = tok.at[blk(z, c, xoff[k])]
        q = k if d > 0 else NX + k
        return send(r, r, z0s.at[q], z0r.at[q], to_u if d > 0 else to_d, y)

    def tz0_got(k, d):
        r = tok.at[blk(zat(-d), c, xoff[k])]
        q = k if d > 0 else NX + k
        send(r, r, z0s.at[q], z0r.at[q], to_u, y).wait_recv()

    def plane(p, cc, n=NX, off=0):
        return tok.at[pl.ds(p * (NX * NC) + cc * NX + off, n)]

    def tz(t, d):
        p = zat(-d * t)
        r = plane(p, c) if t < 3 else plane(p, c, 2, 0 if d > 0 else 2)
        k = t - 1 if d > 0 else 2 + t
        return send(r, r, zs.at[k], zr.at[k], to_u if d > 0 else to_d, y)

    def tz_got(t, d):
        p = zat(-d * (t + 1))
        r = plane(p, c) if t < 3 else plane(p, c, 2, 0 if d > 0 else 2)
        k = t - 1 if d > 0 else 2 + t
        send(r, r, zs.at[k], zr.at[k], to_u, y).wait_recv()

    def across(d, p, cc):
        r = plane(p, cc)
        return send(r, r, ss.at[d], sr.at[d], sib, y)

    def ag(i, k, who, rows, to):
        r = xg.at[i, who] if rows is None else xg.at[i, who, rows]
        return send(r, r, gs.at[k, i], gr.at[k, i], e, to)

    tx(0).start()
    tx(1).start()
    tz0(0, 1).start()
    tz0(0, -1).start()
    ag(NZ, 0, y, None, yu).start()
    ag(NZ, 1, y, None, yd).start()
    wide = jnp.concatenate([router[...], jnp.zeros((ROWS - NE, FEAT), F32)], axis=0)
    lg[3] = lax.dot_general(
        normed32, wide, (((1,), (1,)), ((), ())),
        precision=lax.Precision.HIGHEST, preferred_element_type=F32,
    )
    for k in range(3):
        spread(lg, 3, k).start()
    tx_got(0)
    tx(2).start()
    tz0(3, 1).start()
    tz0(3, -1).start()
    tx_got(1)
    tx(3).start()
    tz0(1, 1).start()
    tz0(1, -1).start()
    tx_got(2)
    tx_got(3)
    tz0(2, 1).start()
    tz0(2, -1).start()
    across(0, z, c).start()
    wz_step(3)

    def ring(t):
        for d in (1, -1):
            if t == 1:
                for k in (0, 3, 1, 2):
                    tz0_got(k, d)
            else:
                tz_got(t - 1, d)
            if t < 4:
                tz(t, d).start()
                p = zat(-d * t)
                across((-d * t) % NZ, p, c).start()
        if t == 4:
            across(4, far, c).start()

    def offset_of(k):
        return lax.shift_right_logical(jnp.int32(ORDER), 3 * k) & 7

    def plane_of(k):
        return lax.rem(z + offset_of(k), NZ)

    def stage_rows(i):
        p = plane_of(i)
        across(offset_of(i), p, 1 - c).wait_recv()
        rows = lax.broadcasted_iota(jnp.int32, (CHUNK, ROWS), 0).astype(F32)
        total = jnp.zeros((CHUNK, FEAT), F32)
        for b in range(0, NX * NC, 2):
            k = p * (NX * NC) + b
            onehot = jnp.concatenate(
                [
                    (rows == slot[pl.ds(k + h, 1), :] + float(CAP * (b + h))).astype(F32)
                    for h in range(2)
                ],
                axis=1,
            ).astype(BF16)
            pair = tok[pl.ds(k, 2)].reshape(2 * ROWS, FEAT)
            total = total + jnp.dot(onehot, pair, preferred_element_type=F32)
        xg[i, y] = total.astype(BF16)
        ag(i, 0, y, None, yu).start()
        ag(i, 1, y, None, yd).start()

    def stage_relay(i):
        ag(i, 0, yd, None, yu).wait_recv()
        ag(i, 2, yd, lo, yu).start()
        ag(i, 1, yu, None, yd).wait_recv()
        ag(i, 3, yu, hi, yd).start()

    def rs1(i, k):
        rows, to = (lo, yu) if k == 0 else (hi, yd)
        return send(pb.at[i, yo, rows], r1.at[i, k], ps.at[k, i], pr.at[k, i], e, to)

    def rs2(i, k):
        to = yu if k == 0 else yd
        return send(pb.at[i, to], r2.at[i, k], ps.at[2 + k, i], pr.at[2 + k, i], e, to)

    def gated(gate, value):
        return (gate / (1.0 + jnp.exp(-gate)) * value).astype(BF16)

    def stage_experts(i):
        ag(i, 2, yo, lo, yu).wait_recv()
        ag(i, 3, yo, hi, yd).wait_recv()
        both = []
        for h in range(2):
            total = jnp.zeros((CHUNK, QPAD), F32)
            for k in range(NY):
                total = total + nt(xg[i, k], wi[h, :, k * FEAT : (k + 1) * FEAT])
            both.append(total)
        hidden = gated(both[0], both[1])

        def down(k, carry):
            d = lax.rem(yo + k, NY)
            w = wo[:, pl.ds(pl.multiple_of(d * FEAT, FEAT), FEAT)]
            pb[i, d] = jnp.dot(hidden, w, preferred_element_type=F32).astype(BF16)
            return carry

        lax.fori_loop(0, 1, down, 0)
        rs1(i, 0).start()
        rs1(i, 1).start()
        lax.fori_loop(1, NY, down, 0)

    def stage_shared():
        ag(NZ, 2, yo, lo, yu).wait_recv()
        ag(NZ, 3, yo, hi, yd).wait_recv()
        for k in range(NX):
            wsib(k, 1 - c).wait_recv()
        acc[...] = jnp.zeros((ROWS, 2 * SPAD), F32)

        def into(zz, carry):
            w = jnp.concatenate(
                [
                    wb[wblk(zz, cc, xx), :, pl.ds(0, 2 * SPAD)]
                    for xx in range(NX)
                    for cc in range(NC)
                ],
                axis=0,
            )
            off = pl.multiple_of(lax.rem(zz, 2) * 256, 256)
            acc[...] += jnp.dot(
                xg[NZ, lax.div(zz, 2), pl.ds(0, ROWS), pl.ds(off, 256)],
                w,
                preferred_element_type=F32,
            )
            return carry

        lax.fori_loop(0, NZ, into, 0)
        hidden = gated(acc[:, :SPAD], acc[:, SPAD:])

        def project(k, carry):
            d = lax.rem(yo + k, NY)
            w = jnp.concatenate(
                [
                    wb[wblk(2 * d + zz, cc, xx), :, pl.ds(2 * SPAD, SPAD)]
                    for zz in range(2)
                    for xx in range(NX)
                    for cc in range(NC)
                ],
                axis=0,
            )
            pb[NZ, d, pl.ds(0, ROWS)] = nt(hidden, w).astype(BF16)
            pb[NZ, d, pl.ds(ROWS, CHUNK - ROWS)] = jnp.zeros((CHUNK - ROWS, FEAT), BF16)
            return carry

        lax.fori_loop(0, NY, project, 0)
        rs1(NZ, 0).start()
        rs1(NZ, 1).start()

    def stage_reduce(i):
        rs1(i, 0).wait_recv()
        pb[i, yu, lo] = (pb[i, yu, lo].astype(F32) + r1[i, 0].astype(F32)).astype(BF16)
        rs2(i, 0).start()
        rs1(i, 1).wait_recv()
        pb[i, yd, hi] = (pb[i, yd, hi].astype(F32) + r1[i, 1].astype(F32)).astype(BF16)
        rs2(i, 1).start()

    def back(i, b):
        to = eid(plane_of(i), lax.rem(b, NX), lax.div(b, NX))
        return to, send(sbuf.at[i, b], rbuf.at[e], os_.at[i * (NX * NC) + b], or_.at[e], to, y)

    def reduced(i):
        rs2(i, 0).wait_recv()
        rs2(i, 1).wait_recv()
        return pb[i, y].astype(F32) + r2[i, 0].astype(F32) + r2[i, 1].astype(F32)

    def stage_return(i):
        total = reduced(i).astype(BF16)
        to_row = lax.broadcasted_iota(jnp.int32, (ROWS, CHUNK), 0)
        of_row = lax.broadcasted_iota(jnp.int32, (ROWS, CHUNK), 1)
        base = CAP * lax.shift_right_logical(to_row, 4)
        inner = to_row & (PACK - 1)

        def move(hit, values):
            return jnp.dot(hit.astype(F32).astype(BF16), values, preferred_element_type=F32)

        first = move(of_row == base + inner, total)
        sbuf[i, :, :, pl.ds(0, FEAT)] = first.astype(BF16).reshape(NX * NC, PACK, FEAT)
        last = jnp.zeros((ROWS, ROWS), F32)
        for q in range(4):
            hit = (of_row == base + PACK + inner - 4 * q) & (inner >= 4 * q) & (inner < 4 * q + 4)
            last = last + move(hit, total[:, q * 128 : (q + 1) * 128])
        sbuf[i, :, :, pl.ds(FEAT, 128)] = last.astype(BF16).reshape(NX * NC, PACK, 128)

        def go(b, carry):
            to, copy = back(i, b)

            @pl.when(to != e)
            def _():
                copy.start()

            @pl.when(to == e)
            def _():
                rbuf[e] = sbuf[i, b]

            return carry

        lax.fori_loop(0, NX * NC, go, 0)

    def stage_tables():
        for k in range(3):
            spread(lg, 3, k).wait_recv()
        logits = (lg[0] + lg[1]) + (lg[2] + lg[3])
        mine = jnp.transpose(names)
        lane = c_i.astype(F32)
        count = jnp.zeros((ROWS, ROWS), F32)
        for k in range(TOP):
            count = count + (mine[:, k : k + 1] == lane).astype(F32)
        chosen = count > 0.5
        top = jnp.max(jnp.where(chosen, logits, -jnp.inf), axis=1, keepdims=True)
        weight = jnp.where(chosen, jnp.exp(jnp.where(chosen, logits - top, 0.0)), 0.0)
        gates = weight / jnp.sum(weight, axis=1, keepdims=True)
        place = jnp.dot(
            (c_i < r_i).astype(F32).astype(BF16), count.astype(BF16), preferred_element_type=F32
        )
        place = jnp.where(chosen, place, 255.0).astype(BF16)
        high = gates.astype(BF16)
        low = (gates - high.astype(F32)).astype(BF16)

        def fill(b, carry):
            ee = lax.broadcasted_iota(jnp.int32, (ROWS, 256), 0)
            jj = lax.broadcasted_iota(jnp.int32, (ROWS, 256), 1)
            inner = jj & (PACK - 1)
            mat = (ee == lax.shift_right_logical(jj, 4) + b * PACK).astype(F32).astype(BF16)
            where = jnp.dot(place, mat, preferred_element_type=F32)
            at = pl.ds(pl.multiple_of(b * 256, 256), 256)
            for h, g in enumerate((high, low)):
                spaced = jnp.dot(g, mat, preferred_element_type=F32)
                for q, want in enumerate((inner, PACK + (inner & 3))):
                    hit = jnp.where(where == want.astype(F32), spaced, 0.0)
                    tab[q, pl.ds(h * ROWS, ROWS), at] = hit.astype(BF16)
            return carry

        lax.fori_loop(0, NE * PACK // 256, fill, 0)

    def step(j, carry):
        @pl.when(j < NZ)
        def _():
            stage_rows(j)

        @pl.when(j == 0)
        def _():
            stage_relay(NZ)
            for d in (1, -1):
                wz_got(3, d)
            wx(0).start()
            wx(1).start()
            wsib(0, c).start()
            for load in loads:
                load.wait()

        @pl.when(j == 3)
        def _():
            wx_got(0)
            wx(2).start()
            wx_got(1)
            wx(3).start()
            wsib(3, c).start()
            wsib(1, c).start()

        @pl.when(j == 5)
        def _():
            wx_got(2)
            wx_got(3)
            wsib(2, c).start()

        @pl.when((j >= 1) & (j < NZ + 1))
        def _():
            stage_relay(j - 1)

        @pl.when((j >= 2) & (j < NZ + 2))
        def _():
            stage_experts(j - 2)

        @pl.when((j >= 3) & (j < NZ + 3))
        def _():
            stage_reduce(j - 3)

        @pl.when(j >= 4)
        def _():
            stage_return(j - 4)

        @pl.when(j == 1)
        def _():
            stage_tables()

        @pl.when(j == SHARED_AT)
        def _():
            stage_shared()

        @pl.when(j == SHARED_AT + 1)
        def _():
            stage_reduce(NZ)

        @pl.when(j == SHARED_AT + 2)
        def _():
            shared[...] = reduced(NZ)[:ROWS]

        for t, at in ((1, 0), (2, 2), (3, 3), (4, 4)):

            @pl.when(j == at)
            def _(t=t):
                ring(t)

        return carry

    lax.fori_loop(0, NZ + 4, step, 0)

    def arrive(k, carry):
        s = lax.rem(e + k, NE)
        send(rbuf.at[s], rbuf.at[s], os_.at[0], or_.at[s], sib, y).wait_recv()
        return carry

    lax.fori_loop(1, NE, arrive, 0)
    back_rows = rbuf[:, :, pl.ds(0, FEAT)].reshape(NE * PACK, FEAT)
    pieces = rbuf[:, :, pl.ds(FEAT, 128)].reshape(NE * PACK, 128).astype(F32)
    part_of = lax.shift_right_logical(
        lax.broadcasted_iota(jnp.int32, (NE * PACK, 128), 0) & (PACK - 1), 2
    )
    extra = jnp.concatenate(
        [jnp.where(part_of == q, pieces, 0.0).astype(BF16) for q in range(4)], axis=1
    )
    both = jnp.dot(tab[0], back_rows, preferred_element_type=F32) + jnp.dot(
        tab[1], extra, preferred_element_type=F32
    )
    out[...] = mixed[...] + (both[:ROWS] + both[ROWS:]) + shared[...]

    for k in range(3):
        ax(k).wait_send()
        spread(sq, 0, k).wait_send()
        spread(lg, 3, k).wait_send()
    for t in range(4):
        for d in (1, -1):
            az(t, d).wait_send()
            if t < 3 or d > 0:
                bz(t, d).wait_send()
            wz(t, d).wait_send()
            tz0(t, d).wait_send()
            if t > 0:
                tz(t, d).wait_send()
        bx(t).wait_send()
        b_sib(t, c).wait_send()
        wx(t).wait_send()
        wsib(t, c).wait_send()
        tx(t).wait_send()
    for d in (0, -1, 1, -2, 2, -3, 3, 4):
        a_sib(d, c).wait_send()
    for k in range(2):
        pa(k).wait_send()
        pb2(k).wait_send()

    def drain(i, carry):
        @pl.when(i < NZ)
        def _():
            across(i, lax.rem(z + i, NZ), c).wait_send()

            def sent(b, inner):
                to, copy = back(i, b)

                @pl.when(to != e)
                def _():
                    copy.wait_send()

                return inner

            lax.fori_loop(0, NX * NC, sent, 0)

        ag(i, 0, y, None, yu).wait_send()
        ag(i, 1, y, None, yd).wait_send()
        ag(i, 2, yd, lo, yu).wait_send()
        ag(i, 3, yu, hi, yd).wait_send()
        for k in range(2):
            rs1(i, k).wait_send()
            rs2(i, k).wait_send()
        return carry

    lax.fori_loop(0, NCH, drain, 0)


def mixer(ctx, opt, ids, hid, gain, router, wsh, win, wout):
    vm = pl.BlockSpec(memory_space=pltpu.VMEM)
    hbm = pl.BlockSpec(memory_space=pl.ANY)

    def pairs(*shapes):
        return [pltpu.SemaphoreType.DMA(s) for s in shapes for _ in range(2)]

    return pl.pallas_call(
        mixer_kernel,
        name="mixer_tail",
        out_shape=jax.ShapeDtypeStruct((ROWS, FEAT), F32),
        in_specs=[vm] * 7 + [hbm] * 2,
        out_specs=vm,
        scratch_shapes=[
            pltpu.VMEM((NE, 16, FEAT + ROWS), BF16),
            pltpu.VMEM((NE, 16, FEAT), BF16),
            pltpu.VMEM((NY, ROWS, FEAT), F32),
            pltpu.VMEM((2, ROWS // 2, FEAT), F32),
            pltpu.VMEM((2, ROWS, FEAT), F32),
            pltpu.VMEM((4, 8, ROWS), F32),
            pltpu.VMEM((4, ROWS, ROWS), F32),
            pltpu.VMEM((ROWS, FEAT), F32),
            pltpu.VMEM((ROWS, FEAT), F32),
            pltpu.VMEM((2, 2 * ROWS, NE * PACK), BF16),
            pltpu.VMEM((NE, ROWS, FEAT), BF16),
            pltpu.VMEM((NE, ROWS), F32),
            pltpu.VMEM((NCH, NY, CHUNK, FEAT), BF16),
            pltpu.VMEM((NCH, NY, CHUNK, FEAT), BF16),
            pltpu.VMEM((NCH, 2, HALF, FEAT), BF16),
            pltpu.VMEM((NCH, 2, CHUNK, FEAT), BF16),
            pltpu.VMEM((NE, 32, 3 * SPAD), BF16),
            pltpu.VMEM((2, QPAD, WIDTH), BF16),
            pltpu.VMEM((QPAD, WIDTH), BF16),
            pltpu.VMEM((NZ, NX * NC, PACK, PWIDTH), BF16),
            pltpu.VMEM((NE, PACK, PWIDTH), BF16),
            pltpu.VMEM((ROWS, 2 * SPAD), F32),
            pltpu.SemaphoreType.DMA((3,)),
        ]
        + pairs((3,), (8,), (8,), (8,), (4,), (4,), (4,), (6,))
        + pairs((4,), (8,), (6,), (8,), (8,), (4,), (4,))
        + pairs((4, NCH), (4, NCH), (NE,)),
        compiler_params=pltpu.CompilerParams(
            collective_id=0, has_side_effects=True, vmem_limit_bytes=VMEM_LIMIT
        ),
    )(ctx, opt, ids, hid, gain, router, wsh, win, wout)


def per_device(
    hidden_state, context, out_proj, norm_gain, router_weight,
    expert_in, expert_out, shared_in, shared_out, route_ids,
):
    gap = ((0, 0), (0, 0), (0, SPAD - SWIDTH))
    shard = jnp.concatenate(
        [
            jnp.pad(shared_in, gap).reshape(32, 2 * SPAD),
            jnp.pad(shared_out.T, ((0, 0), (0, SPAD - SWIDTH))),
        ],
        axis=1,
    )
    win = jnp.transpose(expert_in[0], (1, 2, 0))
    return mixer(
        context, out_proj.T, route_ids.T, hidden_state, norm_gain[None, :],
        router_weight.T, shard, win, expert_out[0],
    )


def solution(mesh):
    return jax.shard_map(
        per_device,
        mesh=mesh,
        in_specs=(
            P("expert", "mp"),
            P("expert", "mp"),
            P("mp", "expert"),
            P("mp"),
            P("mp", None),
            P("expert", None, None, "mp"),
            P("expert", "mp", None),
            P("expert", None, "mp"),
            P("mp", "expert"),
            P("expert", None),
        ),
        out_specs=P("expert", "mp"),
        check_vma=False,
    )
```

time: 549 us -> 195 us (0.36)
  waiting for transfers between devices: 326 us -> 0 us
  Pallas kernels: 0 us -> 189 us
  blocking collectives: 82.6 us -> 0 us
  local copies, waits for them, and re-layouts: 78.1 us -> 3.91 us
  matrix products: 23.6 us -> 0 us
  between operations: 13.8 us -> 0.02 us
  starting transfers between devices: 11.2 us -> 0 us
  other arithmetic: 9.94 us -> 1.47 us
    pallas_call x0 -> x1, Pallas kernels: none -> 189 us  [mixer(): pl.pallas_call(mixer_kernel, name='mixer_tail', out_shape=jax.ShapeDtypeS...]
    all_to_all x1 -> x0, waiting for transfers between devices: 158 us -> none  [per_device(): lax.all_to_all(partial_out, 'expert', split_axis=0, concat_axis=0, tiled=...]
    all_gather x4 -> x0, waiting for transfers between devices: 147 us -> none  [the longest x1 84.3 us: per_device(): lax.all_gather(out_proj, 'expert', axis=1, tiled=True)]
    all_to_all x1 -> x0, blocking collectives: 52.8 us -> none  [per_device(): lax.all_to_all(outgoing, 'expert', split_axis=0, concat_axis=0, tiled=True)]
    reshape x4 -> x0, local copies, waits for them, and re-layouts: 29.5 us -> none  [the longest x1 8.99 us: per_device(): lax.all_gather(incoming, 'mp', axis=2, tiled=True)]
    gather x8 -> x0, local copies, waits for them, and re-layouts: 23.8 us -> none  [the longest x1 10.3 us: per_device(): picked = result.reshape(experts * capacity, result.shape[2])[slot_of]]
    dot_general x6 -> x0, matrix products: 23.6 us -> none  [the longest x1 6.51 us: per_device(): jnp.dot(gathered, weights_in, preferred_element_type=jnp.float32)]
    psum x2 -> x0, blocking collectives: 19.1 us -> none  [the longest x1 12.5 us: per_device(): lax.psum(jnp.dot(normed32, router_weight, precision=lax.Precision.HIGHEST...]
  transfers between devices with their start and end apart: 8 -> 0, of which waited for: 5 -> 0; matrix products, arithmetic and copies ran while one was open for 17% -> 0% of each run, Pallas kernels for 0% -> 0%
where the time goes in v2:
time: 195 us
  Pallas kernels  189 us (97%)
  local copies, waits for them, and re-layouts  3.91 us (2%)
    pallas_call x1, Pallas kernels, mixer(): pl.pallas_call(mixer_kernel, name='mixer_tail', out_shape=jax.ShapeDtypeS...  189 us

profile of v2, /device:TPU:1, one launch (start us, length us, event | category | flops | bytes accessed | tf_op | source)
XLA Modules:
  0.0 194.6 jit_solution(10170319651956062763)
XLA Ops:
  0.0 1.3 broadcast_in_dim.3.gain
  1.3 1.0 pad.8
  2.3 1.5 fusion.1.wsh
  3.7 189.2 %mixer_tail.1 = f32[128,512]{1,0:T(8,128)} custom-call(bf16[128,512]{1,0:T(8,128)(2,1)} %ctx.1, bf16[32,512]{1,0:T(8,128)(2,1)} %bitcast.16, s32[6,128]{1,0:T(8,128)} %bitcast.17, bf16[128,512]{1,0:T(8,128)(2,1)} %hid.1, bf16[1,512]{1,0:T(2,128)(2,1)} %broadcast_in_dim.3.gain, f32[64,512]{1,0:T(8,128)} %bitcast.14, bf16[32,2304]{1,0:T(8,128)(2,1)} %fusion.1.wsh, ...), custom_call_target="tpu_custom_call" | custom-call | tf_op jit(solution)/shard_map/mixer_tail/pallas_call | solution.py:792
  192.9 1.7 copy.13
  (1 shorter events, 0.0 us)

commit v3 on v2

--- a/solution.py
+++ b/solution.py
@@ -9,13 +9,13 @@
 NE = NZ * NX * NC
 ROWS, FEAT, WIDTH = 128, 512, 2048
 TOP, CAP, PACK, PWIDTH = 6, 20, 16, 640
-QUARTER, QPAD = 352, 384
+QUARTER, QPAD = 352, 768
+EIGHTH = QUARTER // 2
 SWIDTH, SPAD = 704, 768
 CHUNK = NX * NC * CAP
 HALF = CHUNK // 2
-NCH = NZ + 1
-SHARED_AT = 7
-ORDER = sum(d << (3 * k) for k, d in enumerate((0, 7, 1, 6, 5, 4, 3, 2)))
+SHARED_AT = 8
+ORDER = sum(d << (3 * k) for k, d in enumerate((0, 7, 1, 2, 5, 4, 3, 6)))
 F32, BF16 = jnp.float32, jnp.bfloat16
 VMEM_LIMIT = 64 * 1024 * 1024 - 65536
 
@@ -63,15 +63,16 @@
 
 def mixer_kernel(
     ctx, opt, ids, hid, gain, router, wsh, win, wout,
-    out,
+    out, base_o,
     wga, wgb, part, p1, p2, sq, lg, mixed, shared, tab,
-    tok, slot, xg, pb, r1, r2, wb, wi, wo, sbuf, rbuf, acc,
+    tok, slot, xo, xg, tr, pb, ra, rb, tq, xsh, psh, s1, s2,
+    wb, wi, wo, sbuf, rbuf, acc, tot,
     wsem,
     axs, axr, azs, azr, ass, asr, bzs, bzr, bxs, bxr, bss, bsr,
     ys, yr, qs, qr,
     xs, xr, z0s, z0r, zs, zr, ss, sr,
     wzs, wzr, wxs, wxr, wss, wsr,
-    gs, gr, ps, pr, os_, or_,
+    hs, hr, gs, gr, ps, pr, vs, vr, os_, or_,
 ):
     e, z, x, c, y = coords()
     xr_, xl_, xo_ = lax.rem(x + 1, NX), lax.rem(x + NX - 1, NX), lax.rem(x + 2, NX)
@@ -79,7 +80,12 @@
     to_u, to_d = eid(lax.rem(z + 1, NZ), x, c), eid(lax.rem(z + NZ - 1, NZ), x, c)
     sib = eid(z, x, 1 - c)
     yu, yd, yo = lax.rem(y + 1, NY), lax.rem(y + NY - 1, NY), lax.rem(y + 2, NY)
-    lo, hi = pl.ds(0, HALF), pl.ds(HALF, HALF)
+    left_, right_ = pl.ds(0, 256), pl.ds(256, 256)
+    par = lax.rem(y, 2)
+    mine = pl.ds(pl.multiple_of(par * HALF, 16), HALF)
+    other = pl.ds(pl.multiple_of((1 - par) * HALF, 16), HALF)
+    near = y + 1 - 2 * par
+    next_ = lax.rem(y + 3 + 2 * par, NY)
     far = lax.rem(z + 4, NZ)
 
     def zat(d):
@@ -114,6 +120,19 @@
     wb[wown] = wsh[...]
     pl.semaphore_wait(pltpu.get_barrier_semaphore(), NE + 2)
 
+    def pair(k):
+        src, dst, at, to, n, where = (
+            (win.at[0], wi.at[0], 0, near, EIGHTH, QUARTER),
+            (win.at[0], wi.at[0], EIGHTH, next_, EIGHTH, QUARTER + EIGHTH),
+            (win.at[1], wi.at[1], 0, near, 80, QUARTER),
+            (win.at[1], wi.at[1], EIGHTH, next_, 80, QUARTER + EIGHTH),
+            (win.at[1], wi.at[1], 80, near, EIGHTH - 80, QUARTER + 80),
+            (win.at[1], wi.at[1], EIGHTH + 80, next_, EIGHTH - 80, QUARTER + EIGHTH + 80),
+            (wout, wo, 0, near, EIGHTH, QUARTER),
+            (wout, wo, EIGHTH, next_, EIGHTH, QUARTER + EIGHTH),
+        )[k]
+        return send(src.at[pl.ds(at, n)], dst.at[pl.ds(where, n)], hs.at[k], hr.at[k], e, to)
+
     def ax(k):
         b, to = [(own, to_r), (own, to_l), (blk(z, c, xl_), to_r)][k]
         return send(wga.at[b], wga.at[b], axs.at[k], axr.at[k], to, y)
@@ -171,6 +190,8 @@
         r = b_col(xoff[k], cc)
         return send(r, r, bss.at[k], bsr.at[k], sib, y)
 
+    for k in range(4):
+        pair(k).start()
     ax(0).start()
     ax(1).start()
     bz(0, 1).start()
@@ -320,11 +341,10 @@
         named.astype(BF16), (r_i < c_i).astype(F32).astype(BF16), preferred_element_type=F32
     )
     slot[...] = jnp.where(named > 0.5, rank, -1000.0)
-    gap = pl.ds(QUARTER, QPAD - QUARTER)
-    wi[0, gap] = jnp.zeros((QPAD - QUARTER, WIDTH), BF16)
-    wi[1, gap] = jnp.zeros((QPAD - QUARTER, WIDTH), BF16)
-    wo[gap] = jnp.zeros((QPAD - QUARTER, WIDTH), BF16)
-    xg[NZ, y, pl.ds(ROWS, CHUNK - ROWS)] = jnp.zeros((CHUNK - ROWS, FEAT), BF16)
+    gap = pl.ds(2 * QUARTER, QPAD - 2 * QUARTER)
+    wi[0, gap] = jnp.zeros((QPAD - 2 * QUARTER, WIDTH), BF16)
+    wi[1, gap] = jnp.zeros((QPAD - 2 * QUARTER, WIDTH), BF16)
+    wo[gap] = jnp.zeros((QPAD - 2 * QUARTER, WIDTH), BF16)
 
     pb2(0).wait_recv()
     pb2(1).wait_recv()
@@ -340,6 +360,8 @@
     sq[3] = jnp.transpose(sums)[:8]
     for k in range(3):
         spread(sq, 0, k).start()
+    for k in range(4, 8):
+        pair(k).start()
     wz_step(2)
     for k in range(3):
         spread(sq, 0, k).wait_recv()
@@ -347,7 +369,7 @@
     inverse = jnp.transpose(jnp.broadcast_to(inverse[:1], (ROWS, ROWS)))[:, :1]
     normed32 = mix * inverse * gain[...].astype(F32)
     tok[own] = normed32.astype(BF16)
-    xg[NZ, y, pl.ds(0, ROWS)] = normed32.astype(BF16)
+    xsh[y] = normed32.astype(BF16)
 
     def tx(k):
         half = ROWS // 2
@@ -395,16 +417,47 @@
         r = plane(p, cc)
         return send(r, r, ss.at[d], sr.at[d], sib, y)
 
-    def ag(i, k, who, rows, to):
-        r = xg.at[i, who] if rows is None else xg.at[i, who, rows]
-        return send(r, r, gs.at[k, i], gr.at[k, i], e, to)
+    def ag(i, k, copy=True):
+        src, dst, to = (
+            (xo.at[i, other], xg.at[i, y if copy else yd], yu),
+            (xo.at[i, other], xg.at[i, y if copy else yu], yd),
+            (xo.at[i, mine, left_], tr.at[i, 0], yu),
+            (xo.at[i, mine, right_], tr.at[i, 1], yd),
+            (tr.at[i, 0], xg.at[i, yd if copy else yo, :, left_], yu),
+            (tr.at[i, 1], xg.at[i, yu if copy else yo, :, right_], yd),
+        )[k]
+        return send(src, dst, gs.at[k, i], gr.at[k, i], e, to)
+
+    def rs(i, k):
+        src, dst, to = (
+            (pb.at[i, yu], ra.at[i, 0], yu),
+            (pb.at[i, yd], ra.at[i, 1], yd),
+            (pb.at[i, yo, :, left_], tq.at[i, 0], yu),
+            (pb.at[i, yo, :, right_], tq.at[i, 1], yd),
+            (tq.at[i, 0], rb.at[i, :, left_], yu),
+            (tq.at[i, 1], rb.at[i, :, right_], yd),
+        )[k]
+        return send(src, dst, ps.at[k, i], pr.at[k, i], e, to)
+
+    def sh(k, who=None):
+        src, dst, to = (
+            (xsh.at[y], xsh.at[y if who is None else who], yu),
+            (xsh.at[y], xsh.at[y if who is None else who], yd),
+            (xsh.at[yd, plo], xsh.at[yd if who is None else who, plo], yu),
+            (xsh.at[yu, phi], xsh.at[yu if who is None else who, phi], yd),
+            (psh.at[yo, plo], s1.at[0], yu),
+            (psh.at[yo, phi], s1.at[1], yd),
+            (psh.at[yu], s2.at[0], yu),
+            (psh.at[yd], s2.at[1], yd),
+        )[k]
+        return send(src, dst, vs.at[k], vr.at[k], e, to)
 
     tx(0).start()
     tx(1).start()
     tz0(0, 1).start()
     tz0(0, -1).start()
-    ag(NZ, 0, y, None, yu).start()
-    ag(NZ, 1, y, None, yd).start()
+    sh(0).start()
+    sh(1).start()
     wide = jnp.concatenate([router[...], jnp.zeros((ROWS - NE, FEAT), F32)], axis=0)
     lg[3] = lax.dot_general(
         normed32, wide, (((1,), (1,)), ((), ())),
@@ -425,7 +478,6 @@
     tz0(2, 1).start()
     tz0(2, -1).start()
     across(0, z, c).start()
-    wz_step(3)
 
     def ring(t):
         for d in (1, -1):
@@ -463,33 +515,25 @@
             ).astype(BF16)
             pair = tok[pl.ds(k, 2)].reshape(2 * ROWS, FEAT)
             total = total + jnp.dot(onehot, pair, preferred_element_type=F32)
-        xg[i, y] = total.astype(BF16)
-        ag(i, 0, y, None, yu).start()
-        ag(i, 1, y, None, yd).start()
+        xo[i] = total.astype(BF16)
+        for k in (2, 3, 0, 1):
+            ag(i, k).start()
+        xg[i, y] = xo[i, mine]
 
     def stage_relay(i):
-        ag(i, 0, yd, None, yu).wait_recv()
-        ag(i, 2, yd, lo, yu).start()
-        ag(i, 1, yu, None, yd).wait_recv()
-        ag(i, 3, yu, hi, yd).start()
-
-    def rs1(i, k):
-        rows, to = (lo, yu) if k == 0 else (hi, yd)
-        return send(pb.at[i, yo, rows], r1.at[i, k], ps.at[k, i], pr.at[k, i], e, to)
-
-    def rs2(i, k):
-        to = yu if k == 0 else yd
-        return send(pb.at[i, to], r2.at[i, k], ps.at[2 + k, i], pr.at[2 + k, i], e, to)
+        for k in (2, 3):
+            ag(i, k, False).wait_recv()
+            ag(i, k + 2).start()
 
     def gated(gate, value):
         return (gate / (1.0 + jnp.exp(-gate)) * value).astype(BF16)
 
     def stage_experts(i):
-        ag(i, 2, yo, lo, yu).wait_recv()
-        ag(i, 3, yo, hi, yd).wait_recv()
+        for k in (0, 1, 4, 5):
+            ag(i, k, False).wait_recv()
         both = []
         for h in range(2):
-            total = jnp.zeros((CHUNK, QPAD), F32)
+            total = jnp.zeros((HALF, QPAD), F32)
             for k in range(NY):
                 total = total + nt(xg[i, k], wi[h, :, k * FEAT : (k + 1) * FEAT])
             both.append(total)
@@ -502,13 +546,15 @@
             return carry
 
         lax.fori_loop(0, 1, down, 0)
-        rs1(i, 0).start()
-        rs1(i, 1).start()
+        rs(i, 2).start()
+        rs(i, 3).start()
         lax.fori_loop(1, NY, down, 0)
+        rs(i, 0).start()
+        rs(i, 1).start()
 
     def stage_shared():
-        ag(NZ, 2, yo, lo, yu).wait_recv()
-        ag(NZ, 3, yo, hi, yd).wait_recv()
+        sh(2, yo).wait_recv()
+        sh(3, yo).wait_recv()
         for k in range(NX):
             wsib(k, 1 - c).wait_recv()
         acc[...] = jnp.zeros((ROWS, 2 * SPAD), F32)
@@ -524,7 +570,7 @@
             )
             off = pl.multiple_of(lax.rem(zz, 2) * 256, 256)
             acc[...] += jnp.dot(
-                xg[NZ, lax.div(zz, 2), pl.ds(0, ROWS), pl.ds(off, 256)],
+                xsh[lax.div(zz, 2), :, pl.ds(off, 256)],
                 w,
                 preferred_element_type=F32,
             )
@@ -544,33 +590,47 @@
                 ],
                 axis=0,
             )
-            pb[NZ, d, pl.ds(0, ROWS)] = nt(hidden, w).astype(BF16)
-            pb[NZ, d, pl.ds(ROWS, CHUNK - ROWS)] = jnp.zeros((CHUNK - ROWS, FEAT), BF16)
+            psh[d] = nt(hidden, w).astype(BF16)
             return carry
 
         lax.fori_loop(0, NY, project, 0)
-        rs1(NZ, 0).start()
-        rs1(NZ, 1).start()
+        sh(4).start()
+        sh(5).start()
 
     def stage_reduce(i):
-        rs1(i, 0).wait_recv()
-        pb[i, yu, lo] = (pb[i, yu, lo].astype(F32) + r1[i, 0].astype(F32)).astype(BF16)
-        rs2(i, 0).start()
-        rs1(i, 1).wait_recv()
-        pb[i, yd, hi] = (pb[i, yd, hi].astype(F32) + r1[i, 1].astype(F32)).astype(BF16)
-        rs2(i, 1).start()
+        for k in (2, 3):
+            rs(i, k).wait_recv()
+            rs(i, k + 2).start()
+
+    def shared_relay():
+        sh(0, yd).wait_recv()
+        sh(2).start()
+        sh(1, yu).wait_recv()
+        sh(3).start()
+
+    def shared_reduce():
+        sh(4).wait_recv()
+        psh[yu, plo] = (psh[yu, plo].astype(F32) + s1[0].astype(F32)).astype(BF16)
+        sh(6).start()
+        sh(5).wait_recv()
+        psh[yd, phi] = (psh[yd, phi].astype(F32) + s1[1].astype(F32)).astype(BF16)
+        sh(7).start()
+
+    def shared_total():
+        sh(6).wait_recv()
+        sh(7).wait_recv()
+        shared[...] = psh[y].astype(F32) + s2[0].astype(F32) + s2[1].astype(F32)
 
     def back(i, b):
         to = eid(plane_of(i), lax.rem(b, NX), lax.div(b, NX))
         return to, send(sbuf.at[i, b], rbuf.at[e], os_.at[i * (NX * NC) + b], or_.at[e], to, y)
 
-    def reduced(i):
-        rs2(i, 0).wait_recv()
-        rs2(i, 1).wait_recv()
-        return pb[i, y].astype(F32) + r2[i, 0].astype(F32) + r2[i, 1].astype(F32)
-
     def stage_return(i):
-        total = reduced(i).astype(BF16)
+        for k in (0, 1, 4, 5):
+            rs(i, k).wait_recv()
+        tot[mine] = pb[i, y].astype(F32) + rb[i].astype(F32)
+        tot[other] = ra[i, 0].astype(F32) + ra[i, 1].astype(F32)
+        total = tot[...].astype(BF16)
         to_row = lax.broadcasted_iota(jnp.int32, (ROWS, CHUNK), 0)
         of_row = lax.broadcasted_iota(jnp.int32, (ROWS, CHUNK), 1)
         base = CAP * lax.shift_right_logical(to_row, 4)
@@ -645,16 +705,18 @@
 
         @pl.when(j == 0)
         def _():
-            stage_relay(NZ)
+            shared_relay()
+            wz_step(3)
+
+        @pl.when(j == 1)
+        def _():
             for d in (1, -1):
                 wz_got(3, d)
             wx(0).start()
             wx(1).start()
             wsib(0, c).start()
-            for load in loads:
-                load.wait()
-
-        @pl.when(j == 3)
+
+        @pl.when(j == 5)
         def _():
             wx_got(0)
             wx(2).start()
@@ -663,7 +725,7 @@
             wsib(3, c).start()
             wsib(1, c).start()
 
-        @pl.when(j == 5)
+        @pl.when(j == 7)
         def _():
             wx_got(2)
             wx_got(3)
@@ -673,6 +735,13 @@
         def _():
             stage_relay(j - 1)
 
+        @pl.when(j == 2)
+        def _():
+            for load in loads:
+                load.wait()
+            for k in range(8):
+                pair(k).wait_recv()
+
         @pl.when((j >= 2) & (j < NZ + 2))
         def _():
             stage_experts(j - 2)
@@ -695,11 +764,11 @@
 
         @pl.when(j == SHARED_AT + 1)
         def _():
-            stage_reduce(NZ)
+            shared_reduce()
 
         @pl.when(j == SHARED_AT + 2)
         def _():
-            shared[...] = reduced(NZ)[:ROWS]
+            shared_total()
 
         for t, at in ((1, 0), (2, 2), (3, 3), (4, 4)):
 
@@ -728,7 +797,8 @@
     both = jnp.dot(tab[0], back_rows, preferred_element_type=F32) + jnp.dot(
         tab[1], extra, preferred_element_type=F32
     )
-    out[...] = mixed[...] + (both[:ROWS] + both[ROWS:]) + shared[...]
+    base_o[...] = mixed[...] + shared[...]
+    out[...] = both[:ROWS] + both[ROWS:]
 
     for k in range(3):
         ax(k).wait_send()
@@ -755,31 +825,27 @@
         pb2(k).wait_send()
 
     def drain(i, carry):
-        @pl.when(i < NZ)
-        def _():
-            across(i, lax.rem(z + i, NZ), c).wait_send()
-
-            def sent(b, inner):
-                to, copy = back(i, b)
-
-                @pl.when(to != e)
-                def _():
-                    copy.wait_send()
-
-                return inner
-
-            lax.fori_loop(0, NX * NC, sent, 0)
-
-        ag(i, 0, y, None, yu).wait_send()
-        ag(i, 1, y, None, yd).wait_send()
-        ag(i, 2, yd, lo, yu).wait_send()
-        ag(i, 3, yu, hi, yd).wait_send()
-        for k in range(2):
-            rs1(i, k).wait_send()
-            rs2(i, k).wait_send()
+        across(i, lax.rem(z + i, NZ), c).wait_send()
+
+        def sent(b, inner):
+            to, copy = back(i, b)
+
+            @pl.when(to != e)
+            def _():
+                copy.wait_send()
+
+            return inner
+
+        lax.fori_loop(0, NX * NC, sent, 0)
+        for k in range(6):
+            ag(i, k).wait_send()
+            rs(i, k).wait_send()
         return carry
 
-    lax.fori_loop(0, NCH, drain, 0)
+    lax.fori_loop(0, NZ, drain, 0)
+    for k in range(8):
+        pair(k).wait_send()
+        sh(k).wait_send()
 
 
 def mixer(ctx, opt, ids, hid, gain, router, wsh, win, wout):
@@ -792,9 +858,9 @@
     return pl.pallas_call(
         mixer_kernel,
         name="mixer_tail",
-        out_shape=jax.ShapeDtypeStruct((ROWS, FEAT), F32),
+        out_shape=[jax.ShapeDtypeStruct((ROWS, FEAT), F32)] * 2,
         in_specs=[vm] * 7 + [hbm] * 2,
-        out_specs=vm,
+        out_specs=[vm] * 2,
         scratch_shapes=[
             pltpu.VMEM((NE, 16, FEAT + ROWS), BF16),
             pltpu.VMEM((NE, 16, FEAT), BF16),
@@ -808,21 +874,29 @@
             pltpu.VMEM((2, 2 * ROWS, NE * PACK), BF16),
             pltpu.VMEM((NE, ROWS, FEAT), BF16),
             pltpu.VMEM((NE, ROWS), F32),
-            pltpu.VMEM((NCH, NY, CHUNK, FEAT), BF16),
-            pltpu.VMEM((NCH, NY, CHUNK, FEAT), BF16),
-            pltpu.VMEM((NCH, 2, HALF, FEAT), BF16),
-            pltpu.VMEM((NCH, 2, CHUNK, FEAT), BF16),
+            pltpu.VMEM((NZ, CHUNK, FEAT), BF16),
+            pltpu.VMEM((NZ, NY, HALF, FEAT), BF16),
+            pltpu.VMEM((NZ, 2, HALF, 256), BF16),
+            pltpu.VMEM((NZ, NY, HALF, FEAT), BF16),
+            pltpu.VMEM((NZ, 2, HALF, FEAT), BF16),
+            pltpu.VMEM((NZ, HALF, FEAT), BF16),
+            pltpu.VMEM((NZ, 2, HALF, 256), BF16),
+            pltpu.VMEM((NY, ROWS, FEAT), BF16),
+            pltpu.VMEM((NY, ROWS, FEAT), BF16),
+            pltpu.VMEM((2, ROWS // 2, FEAT), BF16),
+            pltpu.VMEM((2, ROWS, FEAT), BF16),
             pltpu.VMEM((NE, 32, 3 * SPAD), BF16),
             pltpu.VMEM((2, QPAD, WIDTH), BF16),
             pltpu.VMEM((QPAD, WIDTH), BF16),
             pltpu.VMEM((NZ, NX * NC, PACK, PWIDTH), BF16),
             pltpu.VMEM((NE, PACK, PWIDTH), BF16),
             pltpu.VMEM((ROWS, 2 * SPAD), F32),
+            pltpu.VMEM((CHUNK, FEAT), F32),
             pltpu.SemaphoreType.DMA((3,)),
         ]
         + pairs((3,), (8,), (8,), (8,), (4,), (4,), (4,), (6,))
         + pairs((4,), (8,), (6,), (8,), (8,), (4,), (4,))
-        + pairs((4, NCH), (4, NCH), (NE,)),
+        + pairs((8,), (6, NZ), (6, NZ), (8,), (NE,)),
         compiler_params=pltpu.CompilerParams(
             collective_id=0, has_side_effects=True, vmem_limit_bytes=VMEM_LIMIT
         ),
@@ -842,10 +916,11 @@
         axis=1,
     )
     win = jnp.transpose(expert_in[0], (1, 2, 0))
-    return mixer(
+    routed, base = mixer(
         context, out_proj.T, route_ids.T, hidden_state, norm_gain[None, :],
         router_weight.T, shard, win, expert_out[0],
     )
+    return base + routed
 
 
 def solution(mesh):

time: 195 us -> 182 us (0.933)
  Pallas kernels: 189 us -> 176 us
    pallas_call x1, Pallas kernels: 189 us -> 176 us  [mixer(): pl.pallas_call(mixer_kernel, name='mixer_tail', out_shape=[jax.ShapeDtype...]
where the time goes in v3:
time: 182 us; the launch traced here: 181 us
  Pallas kernels  176 us (97%)
  other arithmetic  3.24 us (2%)
  local copies, waits for them, and re-layouts  2.25 us (1%)
    pallas_call x1, Pallas kernels, mixer(): pl.pallas_call(mixer_kernel, name='mixer_tail', out_shape=[jax.ShapeDtype...  176 us

profile of v3, /device:TPU:1, one launch (start us, length us, event | category | flops | bytes accessed | tf_op | source)
XLA Modules:
  0.0 181.1 jit_solution(2706676233233383798)
XLA Ops:
  0.0 1.3 broadcast_in_dim.3.gain
  1.3 1.0 pad.8
  2.3 1.5 fusion.1.wsh
  3.7 175.6 %mixer_tail.1 = (f32[128,512]{1,0:T(8,128)}, f32[128,512]{1,0:T(8,128)}) custom-call(bf16[128,512]{1,0:T(8,128)(2,1)} %ctx.1, bf16[32,512]{1,0:T(8,128)(2,1)} %bitcast.16, s32[6,128]{1,0:T(8,128)} %bitcast.17, bf16[128,512]{1,0:T(8,128)(2,1)} %hid.1, bf16[1,512]{1,0:T(2,128)(2,1)} %broadcast_in_dim.3.gain, f32[64,512]{1,0:T(8,128)} %bitcast.14, ...), custom_call_target="tpu_custom_call" | custom-call | tf_op jit(solution)/shard_map/mixer_tail/pallas_call | solution.py:858
  179.3 1.8 add.7
  (1 shorter events, 0.0 us)

commit v4 on v3

--- a/solution.py
+++ b/solution.py
@@ -14,8 +14,9 @@
 SWIDTH, SPAD = 704, 768
 CHUNK = NX * NC * CAP
 HALF = CHUNK // 2
-SHARED_AT = 8
-ORDER = sum(d << (3 * k) for k, d in enumerate((0, 7, 1, 2, 5, 4, 3, 6)))
+SHARED_AT = 7
+BXRIGHT = (True, True, True, False, False, False, False, True)
+ORDER = sum(d << (3 * k) for k, d in enumerate((0, 6, 2, 5, 4, 3, 7, 1)))
 F32, BF16 = jnp.float32, jnp.bfloat16
 VMEM_LIMIT = 64 * 1024 * 1024 - 65536
 
@@ -133,6 +134,8 @@
         )[k]
         return send(src.at[pl.ds(at, n)], dst.at[pl.ds(where, n)], hs.at[k], hr.at[k], e, to)
 
+    xoff = (x, xr_, xo_, xl_)
+
     def ax(k):
         b, to = [(own, to_r), (own, to_l), (blk(z, c, xl_), to_r)][k]
         return send(wga.at[b], wga.at[b], axs.at[k], axr.at[k], to, y)
@@ -141,113 +144,114 @@
         b = blk(z, c, [xl_, xr_, xo_][k])
         send(wga.at[b], wga.at[b], axs.at[k], axr.at[k], to_r, y).wait_recv()
 
-    def a_plane(p, cc, n=NX, off=0):
-        return wga.at[pl.ds(p * (NX * NC) + cc * NX + off, n)]
-
-    def az(t, d):
-        p = zat(-d * t)
-        r = a_plane(p, c) if t < 3 else a_plane(p, c, 2, 0 if d > 0 else 2)
-        k = t if d > 0 else 4 + t
-        return send(r, r, azs.at[k], azr.at[k], to_u if d > 0 else to_d, y)
-
-    def az_got(t, d):
-        p = zat(-d * (t + 1))
-        r = a_plane(p, c) if t < 3 else a_plane(p, c, 2, 0 if d > 0 else 2)
-        k = t if d > 0 else 4 + t
-        send(r, r, azs.at[k], azr.at[k], to_u, y).wait_recv()
+    def az(k, t, d, hop=0):
+        r = wga.at[blk(zat(-d * (t + hop)), c, xoff[k])]
+        q = (t if d > 0 else 4 + t) * NX + k
+        return send(r, r, azs.at[q], azr.at[q], to_u if d > 0 else to_d, y)
+
+    def az_goes(k, t, d):
+        return t < 3 or (k < 2) == (d > 0)
 
     def a_sib(d, cc):
-        r = a_plane(zat(d), cc)
+        r = wga.at[pl.ds(zat(d) * (NX * NC) + cc * NX, NX)]
         return send(r, r, ass.at[d % NZ], asr.at[d % NZ], sib, y)
 
-    def bz(t, d):
-        r = wgb.at[wblk(zat(-d * t), c, x)]
-        k = t if d > 0 else 4 + t
-        return send(r, r, bzs.at[k], bzr.at[k], to_u if d > 0 else to_d, y)
-
-    def bz_got(t, d):
-        r = wgb.at[wblk(zat(-d * (t + 1)), c, x)]
-        k = t if d > 0 else 4 + t
-        send(r, r, bzs.at[k], bzr.at[k], to_u, y).wait_recv()
-
-    def b_col(xx, cc, n=NZ, off=0):
-        return wgb.at[pl.ds(cc * (NX * NZ) + xx * NZ + off, n)]
-
-    def bx(k):
-        r, to = [
-            (b_col(x, c), to_r), (b_col(x, c), to_l),
-            (b_col(xl_, c, 4, 0), to_r), (b_col(xr_, c, 4, 4), to_l),
-        ][k]
-        return send(r, r, bxs.at[k], bxr.at[k], to, y)
-
-    def bx_got(k):
-        r = [b_col(xl_, c), b_col(xr_, c), b_col(xo_, c, 4, 0), b_col(xo_, c, 4, 4)][k]
-        send(r, r, bxs.at[k], bxr.at[k], to_r, y).wait_recv()
-
-    xoff = (x, xr_, xo_, xl_)
+    def bz(t, d, hop=0):
+        r = wgb.at[wblk(zat(-d * (t + hop)), c, x)]
+        q = t if d > 0 else 4 + t
+        return send(r, r, bzs.at[q], bzr.at[q], to_u if d > 0 else to_d, y)
+
+    def bx(q, k, copy=True):
+        right = BXRIGHT[q]
+        src, dst, to = (
+            (x, xl_, to_r), (x, xr_, to_l), (xl_ if right else xr_, xo_, to_r if right else to_l),
+        )[k]
+        r = wgb.at[wblk(lax.rem(z + q, NZ), c, src if copy else dst)]
+        return send(r, r, bxs.at[k, q], bxr.at[k, q], to, y)
 
     def b_sib(k, cc):
-        r = b_col(xoff[k], cc)
+        r = wgb.at[pl.ds(cc * (NX * NZ) + xoff[k] * NZ, NZ)]
         return send(r, r, bss.at[k], bsr.at[k], sib, y)
 
-    for k in range(4):
-        pair(k).start()
-    ax(0).start()
-    ax(1).start()
-    bz(0, 1).start()
-    bz(0, -1).start()
-    ax_got(0)
-    ax(2).start()
-    ax_got(1)
-    bz_got(0, 1)
-    bz(1, 1).start()
-    bz_got(0, -1)
-    bz(1, -1).start()
-    ax_got(2)
-    az(0, 1).start()
-    az(0, -1).start()
-    a_sib(0, c).start()
-    bz_got(1, 1)
-    bz(2, 1).start()
-    bz_got(1, -1)
-    bz(2, -1).start()
-    az_got(0, 1)
-    az(1, 1).start()
-    az_got(0, -1)
-    az(1, -1).start()
-    a_sib(-1, c).start()
-    a_sib(1, c).start()
-    bz_got(2, 1)
-    bz(3, 1).start()
-    bz_got(2, -1)
-    az_got(1, 1)
-    az(2, 1).start()
-    az_got(1, -1)
-    az(2, -1).start()
-    bz_got(3, 1)
-    bx(0).start()
-    bx(1).start()
-    a_sib(-2, c).start()
-    a_sib(2, c).start()
-    b_sib(0, c).start()
-    az_got(2, 1)
-    az(3, 1).start()
-    az_got(2, -1)
-    az(3, -1).start()
-    a_sib(-3, c).start()
-    a_sib(3, c).start()
-    bx_got(0)
-    bx(2).start()
-    bx_got(1)
-    bx(3).start()
-    b_sib(3, c).start()
-    b_sib(1, c).start()
-    az_got(3, 1)
-    az_got(3, -1)
-    a_sib(4, c).start()
-    bx_got(2)
-    bx_got(3)
-    b_sib(2, c).start()
+    pair(0).start()
+    pair(1).start()
+    events = []
+
+    def at(when, *args):
+        events.append((when, len(events), args))
+
+    level = 1.9
+    begun = {0: 0.0, 3: level, 1: level, 2: 2 * level}
+    at(0, "ax", 0)
+    at(0, "ax", 1)
+    at(level, "axl")
+    at(level, "axr")
+    at(2 * level, "axo")
+    for t in range(4):
+        for k, q in ((0, 0), (3, 1), (1, 2), (2, 3)):
+            for d in (1, -1):
+                if az_goes(k, t, d):
+                    at(begun[k] + (t + 1) * level + 0.15 * q, "az", k, t, d)
+    at(begun[2] + 4 * level + 0.5, "asib", 4)
+    for d in (1, -1):
+        at(0, "bz0", d)
+        for t in range(4):
+            if t < 3 or d > 0:
+                at((t + 1) * level, "bz", t, d)
+    for q in range(NZ):
+        seen = min(q, NZ - q) * level
+        at(seen + 0.01, "bx", q)
+        at(seen + level + 0.1, "bxl", q)
+        at(seen + level + 0.1, "bxr", q)
+        at(seen + 2 * level + 0.2, "bxo", q)
+    at(4 * level + 0.02, "bsib", 0)
+    at(5 * level + 0.12, "bsib", 3)
+    at(5 * level + 0.12, "bsib", 1)
+    at(6 * level + 0.22, "bsib", 2)
+    for _, _, (what, *v) in sorted(events):
+        if what == "ax":
+            ax(v[0]).start()
+            if v[0] == 0:
+                az(0, 0, 1).start()
+                az(0, 0, -1).start()
+        elif what in ("axl", "axr", "axo"):
+            n = ("axl", "axr", "axo").index(what)
+            ax_got(n)
+            if n == 0:
+                ax(2).start()
+            k = (3, 1, 2)[n]
+            az(k, 0, 1).start()
+            az(k, 0, -1).start()
+            if n == 2:
+                a_sib(0, c).start()
+        elif what == "az":
+            k, t, d = v
+            az(k, t, d, 1).wait_recv()
+            if t < 3 and az_goes(k, t + 1, d):
+                az(k, t + 1, d).start()
+            if t < 3 and k == 2:
+                a_sib(-d * (t + 1), c).start()
+        elif what == "asib":
+            a_sib(v[0], c).start()
+        elif what == "bz0":
+            bz(0, v[0]).start()
+        elif what == "bz":
+            t, d = v
+            bz(t, d, 1).wait_recv()
+            if t < 2 or (t == 2 and d > 0):
+                bz(t + 1, d).start()
+        elif what == "bx":
+            bx(v[0], 0).start()
+            bx(v[0], 1).start()
+        elif what in ("bxl", "bxr"):
+            n = ("bxl", "bxr").index(what)
+            bx(v[0], n, False).wait_recv()
+            if BXRIGHT[v[0]] == (n == 0):
+                bx(v[0], 2).start()
+        elif what == "bxo":
+            bx(v[0], 2, False).wait_recv()
+        else:
+            b_sib(v[0], c).start()
 
     def wz(t, d):
         r = wb.at[wblk(zat(-d * t), c, x)]
@@ -360,7 +364,7 @@
     sq[3] = jnp.transpose(sums)[:8]
     for k in range(3):
         spread(sq, 0, k).start()
-    for k in range(4, 8):
+    for k in range(2, 8):
         pair(k).start()
     wz_step(2)
     for k in range(3):
@@ -699,9 +703,14 @@
         lax.fori_loop(0, NE * PACK // 256, fill, 0)
 
     def step(j, carry):
-        @pl.when(j < NZ)
-        def _():
-            stage_rows(j)
+        def only(cond, do):
+            @pl.when(cond)
+            def _():
+                do()
+
+        only((j >= 1) & (j < NZ + 1), lambda: stage_relay(j - 1))
+        only(j >= 3, lambda: stage_reduce(j - 3))
+        only(j < NZ, lambda: stage_rows(j))
 
         @pl.when(j == 0)
         def _():
@@ -716,7 +725,7 @@
             wx(1).start()
             wsib(0, c).start()
 
-        @pl.when(j == 5)
+        @pl.when(j == 4)
         def _():
             wx_got(0)
             wx(2).start()
@@ -725,15 +734,13 @@
             wsib(3, c).start()
             wsib(1, c).start()
 
-        @pl.when(j == 7)
+        @pl.when(j == 6)
         def _():
             wx_got(2)
             wx_got(3)
             wsib(2, c).start()
 
-        @pl.when((j >= 1) & (j < NZ + 1))
-        def _():
-            stage_relay(j - 1)
+        only(j == SHARED_AT + 1, shared_reduce)
 
         @pl.when(j == 2)
         def _():
@@ -742,43 +749,16 @@
             for k in range(8):
                 pair(k).wait_recv()
 
-        @pl.when((j >= 2) & (j < NZ + 2))
-        def _():
-            stage_experts(j - 2)
-
-        @pl.when((j >= 3) & (j < NZ + 3))
-        def _():
-            stage_reduce(j - 3)
-
-        @pl.when(j >= 4)
-        def _():
-            stage_return(j - 4)
-
-        @pl.when(j == 1)
-        def _():
-            stage_tables()
-
-        @pl.when(j == SHARED_AT)
-        def _():
-            stage_shared()
-
-        @pl.when(j == SHARED_AT + 1)
-        def _():
-            shared_reduce()
-
-        @pl.when(j == SHARED_AT + 2)
-        def _():
-            shared_total()
-
-        for t, at in ((1, 0), (2, 2), (3, 3), (4, 4)):
-
-            @pl.when(j == at)
-            def _(t=t):
-                ring(t)
-
+        only((j >= 2) & (j < NZ + 2), lambda: stage_experts(j - 2))
+        only(j >= 3, lambda: stage_return(j - 3))
+        only(j == 1, stage_tables)
+        only(j == SHARED_AT, stage_shared)
+        only(j == SHARED_AT + 2, shared_total)
+        for t, when in ((1, 0), (2, 0), (3, 2), (4, 3)):
+            only(j == when, lambda t=t: ring(t))
         return carry
 
-    lax.fori_loop(0, NZ + 4, step, 0)
+    lax.fori_loop(0, NZ + 3, step, 0)
 
     def arrive(k, carry):
         s = lax.rem(e + k, NE)
@@ -806,18 +786,22 @@
         spread(lg, 3, k).wait_send()
     for t in range(4):
         for d in (1, -1):
-            az(t, d).wait_send()
+            for k in range(NX):
+                if az_goes(k, t, d):
+                    az(k, t, d).wait_send()
             if t < 3 or d > 0:
                 bz(t, d).wait_send()
             wz(t, d).wait_send()
             tz0(t, d).wait_send()
             if t > 0:
                 tz(t, d).wait_send()
-        bx(t).wait_send()
         b_sib(t, c).wait_send()
         wx(t).wait_send()
         wsib(t, c).wait_send()
         tx(t).wait_send()
+    for q in range(NZ):
+        for k in range(3):
+            bx(q, k).wait_send()
     for d in (0, -1, 1, -2, 2, -3, 3, 4):
         a_sib(d, c).wait_send()
     for k in range(2):
@@ -894,7 +878,7 @@
             pltpu.VMEM((CHUNK, FEAT), F32),
             pltpu.SemaphoreType.DMA((3,)),
         ]
-        + pairs((3,), (8,), (8,), (8,), (4,), (4,), (4,), (6,))
+        + pairs((3,), (32,), (8,), (8,), (3, NZ), (4,), (4,), (6,))
         + pairs((4,), (8,), (6,), (8,), (8,), (4,), (4,))
         + pairs((8,), (6, NZ), (6, NZ), (8,), (NE,)),
         compiler_params=pltpu.CompilerParams(

time: 182 us -> 201 us (1.10)
  Pallas kernels: 176 us -> 195 us
    pallas_call x1, Pallas kernels: 176 us -> 195 us  [mixer(): pl.pallas_call(mixer_kernel, name='mixer_tail', out_shape=[jax.ShapeDtype...]
where the time goes in v4:
time: 201 us
  Pallas kernels  195 us (97%)
  other arithmetic  3.24 us (2%)
  local copies, waits for them, and re-layouts  2.25 us (1%)
    pallas_call x1, Pallas kernels, mixer(): pl.pallas_call(mixer_kernel, name='mixer_tail', out_shape=[jax.ShapeDtype...  195 us

profile of v4, /device:TPU:1, one launch (start us, length us, event | category | flops | bytes accessed | tf_op | source)
XLA Modules:
  0.0 200.9 jit_solution(6063708316415599301)
XLA Ops:
  0.0 1.3 broadcast_in_dim.3.gain
  1.3 1.0 pad.8
  2.3 1.5 fusion.1.wsh
  3.7 195.4 %mixer_tail.1 = (f32[128,512]{1,0:T(8,128)}, f32[128,512]{1,0:T(8,128)}) custom-call(bf16[128,512]{1,0:T(8,128)(2,1)} %ctx.1, bf16[32,512]{1,0:T(8,128)(2,1)} %bitcast.16, s32[6,128]{1,0:T(8,128)} %bitcast.17, bf16[128,512]{1,0:T(8,128)(2,1)} %hid.1, bf16[1,512]{1,0:T(2,128)(2,1)} %broadcast_in_dim.3.gain, f32[64,512]{1,0:T(8,128)} %bitcast.14, ...), custom_call_target="tpu_custom_call" | custom-call | tf_op jit(solution)/shard_map/mixer_tail/pallas_call | solution.py:842
  199.1 1.8 add.7
  (1 shorter events, 0.0 us)

commit v5 on v3

--- a/solution.py
+++ b/solution.py
@@ -14,8 +14,8 @@
 SWIDTH, SPAD = 704, 768
 CHUNK = NX * NC * CAP
 HALF = CHUNK // 2
-SHARED_AT = 8
-ORDER = sum(d << (3 * k) for k, d in enumerate((0, 7, 1, 2, 5, 4, 3, 6)))
+SHARED_AT = 7
+ORDER = sum(d << (3 * k) for k, d in enumerate((0, 6, 2, 5, 4, 3, 7, 1)))
 F32, BF16 = jnp.float32, jnp.bfloat16
 VMEM_LIMIT = 64 * 1024 * 1024 - 65536
 
@@ -699,9 +699,14 @@
         lax.fori_loop(0, NE * PACK // 256, fill, 0)
 
     def step(j, carry):
-        @pl.when(j < NZ)
-        def _():
-            stage_rows(j)
+        def only(cond, do):
+            @pl.when(cond)
+            def _():
+                do()
+
+        only((j >= 1) & (j < NZ + 1), lambda: stage_relay(j - 1))
+        only(j >= 3, lambda: stage_reduce(j - 3))
+        only(j < NZ, lambda: stage_rows(j))
 
         @pl.when(j == 0)
         def _():
@@ -716,7 +721,7 @@
             wx(1).start()
             wsib(0, c).start()
 
-        @pl.when(j == 5)
+        @pl.when(j == 4)
         def _():
             wx_got(0)
             wx(2).start()
@@ -725,15 +730,13 @@
             wsib(3, c).start()
             wsib(1, c).start()
 
-        @pl.when(j == 7)
+        @pl.when(j == 6)
         def _():
             wx_got(2)
             wx_got(3)
             wsib(2, c).start()
 
-        @pl.when((j >= 1) & (j < NZ + 1))
-        def _():
-            stage_relay(j - 1)
+        only(j == SHARED_AT + 1, shared_reduce)
 
         @pl.when(j == 2)
         def _():
@@ -742,43 +745,16 @@
             for k in range(8):
                 pair(k).wait_recv()
 
-        @pl.when((j >= 2) & (j < NZ + 2))
-        def _():
-            stage_experts(j - 2)
-
-        @pl.when((j >= 3) & (j < NZ + 3))
-        def _():
-            stage_reduce(j - 3)
-
-        @pl.when(j >= 4)
-        def _():
-            stage_return(j - 4)
-
-        @pl.when(j == 1)
-        def _():
-            stage_tables()
-
-        @pl.when(j == SHARED_AT)
-        def _():
-            stage_shared()
-
-        @pl.when(j == SHARED_AT + 1)
-        def _():
-            shared_reduce()
-
-        @pl.when(j == SHARED_AT + 2)
-        def _():
-            shared_total()
-
-        for t, at in ((1, 0), (2, 2), (3, 3), (4, 4)):
-
-            @pl.when(j == at)
-            def _(t=t):
-                ring(t)
-
+        only((j >= 2) & (j < NZ + 2), lambda: stage_experts(j - 2))
+        only(j >= 3, lambda: stage_return(j - 3))
+        only(j == 1, stage_tables)
+        only(j == SHARED_AT, stage_shared)
+        only(j == SHARED_AT + 2, shared_total)
+        for t, when in ((1, 0), (2, 0), (3, 2), (4, 3)):
+            only(j == when, lambda t=t: ring(t))
         return carry
 
-    lax.fori_loop(0, NZ + 4, step, 0)
+    lax.fori_loop(0, NZ + 3, step, 0)
 
     def arrive(k, carry):
         s = lax.rem(e + k, NE)

time: 182 us -> 193 us (1.060)
  Pallas kernels: 176 us -> 187 us
    pallas_call x1, Pallas kernels: 176 us -> 187 us  [mixer(): pl.pallas_call(mixer_kernel, name='mixer_tail', out_shape=[jax.ShapeDtype...]
where the time goes in v5:
time: 193 us
  Pallas kernels  187 us (97%)
  other arithmetic  3.24 us (2%)
  local copies, waits for them, and re-layouts  2.25 us (1%)
    pallas_call x1, Pallas kernels, mixer(): pl.pallas_call(mixer_kernel, name='mixer_tail', out_shape=[jax.ShapeDtype...  187 us

profile of v5, /device:TPU:1, one launch (start us, length us, event | category | flops | bytes accessed | tf_op | source)
XLA Modules:
  0.0 192.5 jit_solution(13724626266893384639)
XLA Ops:
  0.0 1.3 broadcast_in_dim.3.gain
  1.3 1.0 pad.8
  2.3 1.5 fusion.1.wsh
  3.7 187.0 %mixer_tail.1 = (f32[128,512]{1,0:T(8,128)}, f32[128,512]{1,0:T(8,128)}) custom-call(bf16[128,512]{1,0:T(8,128)(2,1)} %ctx.1, bf16[32,512]{1,0:T(8,128)(2,1)} %bitcast.16, s32[6,128]{1,0:T(8,128)} %bitcast.17, bf16[128,512]{1,0:T(8,128)(2,1)} %hid.1, bf16[1,512]{1,0:T(2,128)(2,1)} %broadcast_in_dim.3.gain, f32[64,512]{1,0:T(8,128)} %bitcast.14, ...), custom_call_target="tpu_custom_call" | custom-call | tf_op jit(solution)/shard_map/mixer_tail/pallas_call | solution.py:834
  190.7 1.8 add.7
  (1 shorter events, 0.0 us)

commit v6 on v3

--- a/solution.py
+++ b/solution.py
@@ -62,7 +62,7 @@
 
 
 def mixer_kernel(
-    ctx, opt, ids, hid, gain, router, wsh, win, wout,
+    ctx, opt, ids, hid, gain, router, win_s, wout_s, win, wout,
     out, base_o,
     wga, wgb, part, p1, p2, sq, lg, mixed, shared, tab,
     tok, slot, xo, xg, tr, pb, ra, rb, tq, xsh, psh, s1, s2,
@@ -117,7 +117,10 @@
     wga[own, :, pl.ds(0, FEAT)] = opt[0:16, :]
     wga[own, :, pl.ds(FEAT, ROWS)] = names[:16].astype(BF16)
     wgb[wown] = opt[16:32, :]
-    wb[wown] = wsh[...]
+    none = jnp.zeros((32, SPAD - SWIDTH), BF16)
+    for h in range(3):
+        piece = win_s[:, h, :] if h < 2 else wout_s[...]
+        wb[wown, :, pl.ds(h * SPAD, SPAD)] = jnp.concatenate([piece, none], axis=1)
     pl.semaphore_wait(pltpu.get_barrier_semaphore(), NE + 2)
 
     def pair(k):
@@ -325,6 +328,8 @@
     pa(1).wait_recv()
     part[yd, phi] = part[yd, phi] + p1[1]
     pb2(1).start()
+    pair(4).start()
+    pair(5).start()
     part[y] = columns(y)
     wz_step(1)
 
@@ -360,14 +365,15 @@
     sq[3] = jnp.transpose(sums)[:8]
     for k in range(3):
         spread(sq, 0, k).start()
-    for k in range(4, 8):
+    for k in range(6, 8):
         pair(k).start()
     wz_step(2)
     for k in range(3):
         spread(sq, 0, k).wait_recv()
     inverse = lax.rsqrt(((sq[0] + sq[1]) + (sq[2] + sq[3])) / WIDTH + 1e-06)
     inverse = jnp.transpose(jnp.broadcast_to(inverse[:1], (ROWS, ROWS)))[:, :1]
-    normed32 = mix * inverse * gain[...].astype(F32)
+    gains = jnp.concatenate([gain[k : k + 1] for k in range(4)], axis=1)
+    normed32 = mix * inverse * gains.astype(F32)
     tok[own] = normed32.astype(BF16)
     xsh[y] = normed32.astype(BF16)
 
@@ -699,6 +705,10 @@
         lax.fori_loop(0, NE * PACK // 256, fill, 0)
 
     def step(j, carry):
+        @pl.when((j >= 1) & (j < NZ + 1))
+        def _():
+            stage_relay(j - 1)
+
         @pl.when(j < NZ)
         def _():
             stage_rows(j)
@@ -730,10 +740,6 @@
             wx_got(2)
             wx_got(3)
             wsib(2, c).start()
-
-        @pl.when((j >= 1) & (j < NZ + 1))
-        def _():
-            stage_relay(j - 1)
 
         @pl.when(j == 2)
         def _():
@@ -848,7 +854,7 @@
         sh(k).wait_send()
 
 
-def mixer(ctx, opt, ids, hid, gain, router, wsh, win, wout):
+def mixer(ctx, opt, ids, hid, gain, router, win_s, wout_s, win, wout):
     vm = pl.BlockSpec(memory_space=pltpu.VMEM)
     hbm = pl.BlockSpec(memory_space=pl.ANY)
 
@@ -859,7 +865,7 @@
         mixer_kernel,
         name="mixer_tail",
         out_shape=[jax.ShapeDtypeStruct((ROWS, FEAT), F32)] * 2,
-        in_specs=[vm] * 7 + [hbm] * 2,
+        in_specs=[vm] * 8 + [hbm] * 2,
         out_specs=[vm] * 2,
         scratch_shapes=[
             pltpu.VMEM((NE, 16, FEAT + ROWS), BF16),
@@ -900,25 +906,17 @@
         compiler_params=pltpu.CompilerParams(
             collective_id=0, has_side_effects=True, vmem_limit_bytes=VMEM_LIMIT
         ),
-    )(ctx, opt, ids, hid, gain, router, wsh, win, wout)
+    )(ctx, opt, ids, hid, gain, router, win_s, wout_s, win, wout)
 
 
 def per_device(
     hidden_state, context, out_proj, norm_gain, router_weight,
     expert_in, expert_out, shared_in, shared_out, route_ids,
 ):
-    gap = ((0, 0), (0, 0), (0, SPAD - SWIDTH))
-    shard = jnp.concatenate(
-        [
-            jnp.pad(shared_in, gap).reshape(32, 2 * SPAD),
-            jnp.pad(shared_out.T, ((0, 0), (0, SPAD - SWIDTH))),
-        ],
-        axis=1,
-    )
     win = jnp.transpose(expert_in[0], (1, 2, 0))
     routed, base = mixer(
-        context, out_proj.T, route_ids.T, hidden_state, norm_gain[None, :],
-        router_weight.T, shard, win, expert_out[0],
+        context, out_proj.T, route_ids.T, hidden_state, norm_gain.reshape(4, 128),
+        router_weight.T, shared_in, shared_out.T, win, expert_out[0],
     )
     return base + routed
 

time: 182 us -> 177 us (0.973)
  local copies, waits for them, and re-layouts: 2.25 us -> 0 us
where the time goes in v6:
time: 177 us; the launch traced here: 176 us
  Pallas kernels  175 us (99%)
  other arithmetic  1.77 us (1%)
    pallas_call x1, Pallas kernels, mixer(): pl.pallas_call(mixer_kernel, name='mixer_tail', out_shape=[jax.ShapeDtype...  175 us

profile of v6, /device:TPU:1, one launch (start us, length us, event | category | flops | bytes accessed | tf_op | source)
XLA Modules:
  0.0 176.4 jit_solution(7878409789981211613)
XLA Ops:
  0.0 174.6 %mixer_tail.1 = (f32[128,512]{1,0:T(8,128)}, f32[128,512]{1,0:T(8,128)}) custom-call(bf16[128,512]{1,0:T(8,128)(2,1)} %ctx.1, bf16[32,512]{1,0:T(8,128)(2,1)} %bitcast.13, s32[6,128]{1,0:T(8,128)} %bitcast.14, bf16[128,512]{1,0:T(8,128)(2,1)} %hid.1, bf16[4,128]{1,0:T(4,128)(2,1)} %bitcast.15, f32[64,512]{1,0:T(8,128)} %bitcast.11, ...), custom_call_target="tpu_custom_call" | custom-call | tf_op jit(solution)/shard_map/mixer_tail/pallas_call | solution.py:864
  174.6 1.8 %add.3 = f32[128,512]{1,0:T(8,128)} add(f32[128,512]{1,0:T(8,128)} %get-tuple-element.7, f32[128,512]{1,0:T(8,128)} %get-tuple-element.8) | non-fusion elementwise | flops 65536 | bytes 786432 | tf_op jit(solution)/shard_map/add | solution.py:921

commit v7 on v6

--- a/solution.py
+++ b/solution.py
@@ -715,7 +715,6 @@
 
         @pl.when(j == 0)
         def _():
-            shared_relay()
             wz_step(3)
 
         @pl.when(j == 1)
@@ -747,6 +746,7 @@
                 load.wait()
             for k in range(8):
                 pair(k).wait_recv()
+            shared_relay()
 
         @pl.when((j >= 2) & (j < NZ + 2))
         def _():
@@ -760,7 +760,7 @@
         def _():
             stage_return(j - 4)
 
-        @pl.when(j == 1)
+        @pl.when(j == 5)
         def _():
             stage_tables()
 
@@ -776,7 +776,7 @@
         def _():
             shared_total()
 
-        for t, at in ((1, 0), (2, 2), (3, 3), (4, 4)):
+        for t, at in ((1, 0), (2, 1), (3, 2), (4, 3)):
 
             @pl.when(j == at)
             def _(t=t):

time: 177 us -> 172 us (0.972)
  Pallas kernels: 175 us -> 170 us
    pallas_call x1, Pallas kernels: 175 us -> 170 us  [mixer(): pl.pallas_call(mixer_kernel, name='mixer_tail', out_shape=[jax.ShapeDtype...]
where the time goes in v7:
time: 172 us
  Pallas kernels  170 us (99%)
  other arithmetic  1.77 us (1%)
    pallas_call x1, Pallas kernels, mixer(): pl.pallas_call(mixer_kernel, name='mixer_tail', out_shape=[jax.ShapeDtype...  170 us

profile of v7, /device:TPU:1, one launch (start us, length us, event | category | flops | bytes accessed | tf_op | source)
XLA Modules:
  0.0 171.7 jit_solution(17106342049643272775)
XLA Ops:
  0.0 169.9 %mixer_tail.1 = (f32[128,512]{1,0:T(8,128)}, f32[128,512]{1,0:T(8,128)}) custom-call(bf16[128,512]{1,0:T(8,128)(2,1)} %ctx.1, bf16[32,512]{1,0:T(8,128)(2,1)} %bitcast.13, s32[6,128]{1,0:T(8,128)} %bitcast.14, bf16[128,512]{1,0:T(8,128)(2,1)} %hid.1, bf16[4,128]{1,0:T(4,128)(2,1)} %bitcast.15, f32[64,512]{1,0:T(8,128)} %bitcast.11, ...), custom_call_target="tpu_custom_call" | custom-call | tf_op jit(solution)/shard_map/mixer_tail/pallas_call | solution.py:864
  169.9 1.8 %add.3 = f32[128,512]{1,0:T(8,128)} add(f32[128,512]{1,0:T(8,128)} %get-tuple-element.7, f32[128,512]{1,0:T(8,128)} %get-tuple-element.8) | non-fusion elementwise | flops 65536 | bytes 786432 | tf_op jit(solution)/shard_map/add | solution.py:921

commit v8 on v7

--- a/solution.py
+++ b/solution.py
@@ -15,7 +15,7 @@
 CHUNK = NX * NC * CAP
 HALF = CHUNK // 2
 SHARED_AT = 8
-ORDER = sum(d << (3 * k) for k, d in enumerate((0, 7, 1, 2, 5, 4, 3, 6)))
+ORDER = sum(d << (3 * k) for k, d in enumerate((0, 7, 2, 6, 3, 4, 5, 1)))
 F32, BF16 = jnp.float32, jnp.bfloat16
 VMEM_LIMIT = 64 * 1024 * 1024 - 65536
 

time: 172 us -> 171 us (level)
  no operation moved by 1% of the time
where the time goes in v8:
time: 171 us
  Pallas kernels  170 us (99%)
  other arithmetic  1.77 us (1%)
    pallas_call x1, Pallas kernels, mixer(): pl.pallas_call(mixer_kernel, name='mixer_tail', out_shape=[jax.ShapeDtype...  170 us

profile of v8, /device:TPU:1, one launch (start us, length us, event | category | flops | bytes accessed | tf_op | source)
XLA Modules:
  0.0 171.3 jit_solution(11181377920647192671)
XLA Ops:
  0.0 169.5 %mixer_tail.1 = (f32[128,512]{1,0:T(8,128)}, f32[128,512]{1,0:T(8,128)}) custom-call(bf16[128,512]{1,0:T(8,128)(2,1)} %ctx.1, bf16[32,512]{1,0:T(8,128)(2,1)} %bitcast.13, s32[6,128]{1,0:T(8,128)} %bitcast.14, bf16[128,512]{1,0:T(8,128)(2,1)} %hid.1, bf16[4,128]{1,0:T(4,128)(2,1)} %bitcast.15, f32[64,512]{1,0:T(8,128)} %bitcast.11, ...), custom_call_target="tpu_custom_call" | custom-call | tf_op jit(solution)/shard_map/mixer_tail/pallas_call | solution.py:864
  169.5 1.8 %add.3 = f32[128,512]{1,0:T(8,128)} add(f32[128,512]{1,0:T(8,128)} %get-tuple-element.7, f32[128,512]{1,0:T(8,128)} %get-tuple-element.8) | non-fusion elementwise | flops 65536 | bytes 786432 | tf_op jit(solution)/shard_map/add | solution.py:921
